TPU v7x, 32 devices: a whole 2x2x4 slice. The times are simulated.
32 devices in a mesh: head: 4 (over y, core), seq: 8 (over z, x).
Axes of the slice: x: 2, y: 2, z: 4, core: 2. Of those that a mesh axis runs over, the one named last changes fastest.
Arguments:
- queries: bfloat16 [4096, 4096], P('seq', 'head'), may hold values from -6 to 6
- keys: bfloat16 [4096, 4096], P('seq', 'head'), may hold values from -6 to 6
- values: bfloat16 [4096, 4096], P('seq', 'head'), may hold values from -6 to 6
- rate: float32 [8, 4096], P('head', 'seq'), may hold values from 0.0001 to 0.001
- fast_gate: float32 [8, 512, 512], P('head', 'seq'), may hold values from -3 to 3
- fast_up: float32 [8, 512, 512], P('head', 'seq'), may hold values from -3 to 3
- fast_down: float32 [8, 512, 512], P('head', 'seq'), may hold values from -8 to 8
- out_gain: float32 [4096], P('head'), may hold values from 0.25 to 1.75
Outputs:
- mixed: bfloat16 [4096, 4096], P('seq', 'head')
- new_gate: float32 [8, 512, 512], P('head', 'seq')
- new_up: float32 [8, 512, 512], P('head', 'seq')
- new_down: float32 [8, 512, 512], P('head', 'seq')
All inputs are finite; a program needn't handle non-finite values.
Results may differ from a plain program's by a relative error of at most 0.012.
Values may be sent and summed in bfloat16 or wider, within the bound.
A program may use at most 128 MiB of HBM per device.

v0:
```python
import functools
import math

import jax
import jax.numpy as jnp
from jax import lax
from jax.experimental import pallas as pl
from jax.experimental.pallas import tpu as pltpu
from jax.sharding import PartitionSpec as P

WINDOW = 512
EPS = 1e-06
TILE = 128
MESH = pl.DeviceIdType.MESH
F32 = jnp.float32
BF16 = jnp.bfloat16


def dot(a, b):
    return jnp.dot(a, b, preferred_element_type=F32)


def dot_lhs_t(a, b):
    return lax.dot_general(a, b, (((0,), (0,)), ((), ())), preferred_element_type=F32)


def dot_rhs_t(a, b):
    return lax.dot_general(a, b, (((1,), (1,)), ((), ())), preferred_element_type=F32)


def kernel(
    n, hn,
    q, k, v, rate, gain, w1, w3, w2,
    mixed, o1, o3, o2,
    wg, ug, pg, rs_out, rs_in, wb_out, wf_out, wf_in, own, g_out, g_in, ratio_out, ratio_in,
    qx, kx, vx, eta_x, gv, hid, dab, attn, attn_out, attn_in, branch, f_out, f_in, sq, sq_in,
    ag_s, ag_r, rs_s, rs_r, au_s, au_r, x_s, x_r, halo_s, halo_r, f_s, f_r, sq_s, sq_r,
):
    rows, width = q.shape
    heads, shard, hd = w1.shape
    line = n // 2
    tiles = rows // TILE
    me = lax.axis_index("seq")
    hme = lax.axis_index("head")
    m = lax.div(me, 2)
    c = lax.rem(me, 2)
    oc = 1 - c
    partner = 2 * m + oc
    step_to = (1, -1)
    weights = (w1, w3, w2)

    def seq_at(b):
        return 2 * lax.rem(b + line, line) + c

    def lanes(i):
        return pl.ds(pl.multiple_of(i * hd, hd), hd)

    def block(i):
        return pl.ds(pl.multiple_of(i * rows, rows), rows)

    def after_halo(i):
        return pl.ds(pl.multiple_of(WINDOW + i * rows, TILE), rows)

    barrier = pltpu.get_barrier_semaphore()
    for s in (partner, seq_at(m + 1), seq_at(m - 1)):
        pl.semaphore_signal(barrier, inc=1, device_id={"seq": s}, device_id_type=MESH)
    for d in range(1, hn):
        pl.semaphore_signal(
            barrier, inc=1, device_id={"head": lax.rem(hme + d, hn)}, device_id_type=MESH
        )
    for j, w in enumerate(weights):
        wg[j, m, c] = w[c].astype(BF16)
        wb_out[j] = w[oc].astype(BF16)
        wf_out[j] = w[oc]
    pl.semaphore_wait(barrier, 3 + hn - 1)

    pending = []

    def start(copy, when=None):
        if when is None:
            copy.start()
        else:
            pl.when(when)(copy.start)
        pending.append((copy, when))

    def wait(copy, when):
        pl.when(when)(copy.wait_recv)

    def to_partner(i, src, dst):
        return pltpu.make_async_remote_copy(
            src_ref=src, dst_ref=dst, send_sem=x_s.at[i], recv_sem=x_r.at[i],
            device_id={"seq": partner}, device_id_type=MESH,
        )

    x_w = to_partner(0, wb_out, wg.at[:, m, c])
    x_k = to_partner(1, k.at[:, lanes(oc)], kx.at[after_halo(c)])
    x_v = to_partner(2, v.at[:, lanes(oc)], vx.at[after_halo(c)])
    x_e = to_partner(3, rate, eta_x.at[c])
    x_f = to_partner(4, wf_out, wf_in)
    x_q = to_partner(5, q.at[:, lanes(oc)], qx.at[block(c)])
    x_g = to_partner(6, g_out, g_in)
    x_a = to_partner(7, attn_out, attn_in)
    x_r_ = to_partner(8, ratio_out, ratio_in)
    for x in (x_w, x_k, x_v, x_e, x_f, x_q):
        start(x)

    def link(ss, rr, src, dst, d, j, s):
        return pltpu.make_async_remote_copy(
            src_ref=src, dst_ref=dst, send_sem=ss.at[d, j, s - 1], recv_sem=rr.at[d, j, s - 1],
            device_id={"seq": seq_at(m + step_to[d])}, device_id_type=MESH,
        )

    def ahead(d):
        return line - 1 - m if d == 0 else m

    def gather_copy(buf, ss, rr, d, j, s):
        b = lax.rem(m - step_to[d] * (s - 1) + line, line)
        return link(ss, rr, buf.at[j, b], buf.at[j, b], d, j, s)

    def gather_wait(buf, ss, rr, d, j, s):
        b = lax.rem(m - step_to[d] * s + line, line)
        wait(link(ss, rr, buf.at[j, b], buf.at[j, b], d, j, s), ahead(1 - d) >= s)

    def gather_send(buf, ss, rr, j, s):
        for d in range(2):
            if s > 1:
                gather_wait(buf, ss, rr, d, j, s - 1)
            start(
                gather_copy(buf, ss, rr, d, j, s),
                jnp.logical_and(ahead(d) >= 1, ahead(1 - d) >= s - 1),
            )

    def gather_finish(buf, ss, rr, j):
        for d in range(2):
            gather_wait(buf, ss, rr, d, j, line - 1)

    def reduce_copy(d, j, s):
        return link(rs_s, rs_r, rs_out.at[d, j, s - 1], rs_in.at[d, j, s - 1], d, j, s)

    def reduce_send(j, s, near):
        for d in range(2):
            target = line - s if d == 0 else s - 1
            copy = reduce_copy(d, j, s)
            closer = ahead(1 - d) * 2 < line
            turn = closer if near else jnp.logical_not(closer)
            active = jnp.logical_and(turn, target > m if d == 0 else target < m)
            first = ahead(1 - d) == 0
            if near:

                @pl.when(jnp.logical_and(active, first))
                def _():
                    rs_out[d, j, s - 1] = pg[j, target].astype(BF16)

            @pl.when(jnp.logical_and(active, jnp.logical_not(first)))
            def _():
                copy.wait_recv()
                part = pg[j, target] + rs_in[d, j, s - 1].astype(F32)
                rs_out[d, j, s - 1] = part.astype(BF16)

            start(copy, active)

    def reduce_piece(j):
        for s in range(1, line + 1):
            if s < line:
                reduce_send(j, s, True)
            if s > 1:
                reduce_send(j, s - 1, False)

    def reduce_finish(j):
        own[j] = pg[j, m]
        for d in range(2):
            for s in range(1, line):
                target = line - s if d == 0 else s - 1

                @pl.when(target == m)
                def _():
                    reduce_copy(d, j, s).wait_recv()
                    own[j] = own[j] + rs_in[d, j, s - 1].astype(F32)

        g_out[j] = own[j, oc]
        upd = own[j, c] + weights[j][c]
        own[j, c] = upd
        ug[j, m, c] = upd.astype(BF16)
        ug[j, m, oc] = (own[j, oc] + wf_in[j]).astype(BF16)

    halo = [
        pltpu.make_async_remote_copy(
            src_ref=x.at[2 * rows:2 * rows + WINDOW], dst_ref=x.at[0:WINDOW],
            send_sem=halo_s.at[i], recv_sem=halo_r.at[i],
            device_id={"seq": seq_at(m + 1)}, device_id_type=MESH,
        )
        for i, x in enumerate((kx, vx))
    ]

    def column(row):
        return jnp.transpose(jnp.broadcast_to(row, (TILE, row.shape[1])))

    def full(buf, j):
        return buf[j].reshape(n * shard, hd)

    def gradients():
        @pl.loop(0, 2 * tiles)
        def _(i):
            at = pl.ds(pl.multiple_of(i * TILE, TILE), TILE)
            kt = kx[pl.ds(pl.multiple_of(WINDOW + i * TILE, TILE), TILE), :]
            gt = gv[at, :]
            a = dot(kt, full(wg, 0))
            b = dot(kt, full(wg, 1))
            back = dot_rhs_t(gt, full(wg, 2))
            g = jax.nn.sigmoid(a)
            ag = a * g
            hid[at, :] = (ag * b).astype(BF16)
            dab[0, at, :] = (back * b * g * (1.0 + a * (1.0 - g))).astype(BF16)
            dab[1, at, :] = (back * ag).astype(BF16)

    def product(j):
        if j == 2:
            g = dot_lhs_t(hid[...], gv[...])
        else:
            g = dot_lhs_t(kx[WINDOW:, :], dab[j])
        pg[j] = g.reshape(line, 2, shard, hd)

    def attention(b, out):
        span = WINDOW + TILE

        @pl.loop(0, tiles)
        def _(i):
            base = pl.multiple_of(b * rows + i * TILE, TILE)
            s = dot_rhs_t(qx[pl.ds(base, TILE), :], kx[pl.ds(base, span), :])
            s = s * (1.0 / math.sqrt(hd))
            r = lax.broadcasted_iota(jnp.int32, (TILE, span), 0)
            u = lax.broadcasted_iota(jnp.int32, (TILE, span), 1)
            ok = (u > r) & (u <= r + WINDOW) & (base + u + m * 2 * rows >= WINDOW)
            s = jnp.where(ok, s, -jnp.inf)
            e = jnp.exp(s - jnp.max(s, axis=1, keepdims=True))
            p = (e * (1.0 / jnp.sum(e, axis=1, keepdims=True))).astype(BF16)
            res = dot(p, vx[pl.ds(base, span), :])
            out[pl.ds(pl.multiple_of(i * TILE, TILE), TILE), :] = res.astype(out.dtype)

    def sum_squares(buf, j):
        x = full(buf, j).astype(F32)
        return jnp.sum(x * x, axis=0, keepdims=True)

    def f_copy(i):
        at = pl.ds(pl.multiple_of(i * TILE, TILE), TILE)
        return pltpu.make_async_remote_copy(
            src_ref=f_out.at[at], dst_ref=f_in.at[at], send_sem=f_s.at[i], recv_sem=f_r.at[i],
            device_id={"seq": partner}, device_id_type=MESH,
        )

    def flat(f):
        row_sq = jnp.broadcast_to(jnp.sum(f * f, axis=1, keepdims=True), (TILE, TILE))
        return jnp.transpose(row_sq)[:8]

    def apply_tile(i, b):
        qt = qx[pl.ds(pl.multiple_of(b * rows + i * TILE, TILE), TILE), :]
        a = dot(qt, full(ug, 0)) * ratio_out[0:1]
        g = dot(qt, full(ug, 1)) * ratio_out[1:2]
        hh = (a * jax.nn.sigmoid(a) * g).astype(BF16)
        return dot(hh, full(ug, 2)) * ratio_out[2:3]

    kx[after_halo(c), :] = k[:, lanes(c)]
    vx[after_halo(c), :] = v[:, lanes(c)]
    qx[block(c), :] = q[:, lanes(c)]
    eta_x[c] = rate[...]

    @pl.when(m == 0)
    def _():
        for dst in (kx, vx):
            dst[:WINDOW, :] = jnp.zeros((WINDOW, hd), BF16)

    order_w = (0, 1, 2)
    x_w.wait_recv()
    for j in order_w:
        gather_send(wg, ag_s, ag_r, j, 1)
    for s in range(2, line):
        for j in order_w:
            gather_send(wg, ag_s, ag_r, j, s)
    x_k.wait_recv()
    start(halo[0], m < line - 1)
    x_v.wait_recv()
    start(halo[1], m < line - 1)
    x_e.wait_recv()
    for b in range(2):
        eta = column(eta_x[b, pl.ds(c, 1), :])[:, :1]
        at = slice(b * rows, (b + 1) * rows)
        vb = vx[WINDOW + b * rows:WINDOW + (b + 1) * rows, :]
        gv[at, :] = (eta * vb.astype(F32)).astype(BF16)
    for j in order_w:
        gather_finish(wg, ag_s, ag_r, j)
    gradients()

    def pass_on(j, s):
        if s < line:
            gather_send(ug, au_s, au_r, j, s)

    product(0)
    reduce_piece(0)
    product(1)
    reduce_piece(1)
    product(2)
    x_f.wait_recv()
    reduce_finish(0)
    pass_on(0, 1)
    reduce_piece(2)
    reduce_finish(1)
    pass_on(1, 1)
    pass_on(0, 2)
    reduce_finish(2)
    pass_on(2, 1)
    start(x_g)
    pass_on(1, 2)
    pass_on(0, 3)
    x_q.wait_recv()
    for h in halo:
        wait(h, m > 0)
    attention(oc, attn_out)
    start(x_a)
    pass_on(2, 2)
    pass_on(1, 3)
    attention(c, attn)
    for j in range(3):
        ratio_out[j:j + 1] = jnp.sqrt(sum_squares(wg, j))
    pass_on(2, 3)
    for s in range(4, line):
        for j in order_w:
            pass_on(j, s)
    for j in order_w:
        gather_finish(ug, au_s, au_r, j)
        ratio_out[j:j + 1] = ratio_out[j:j + 1] / jnp.sqrt(sum_squares(ug, j) + EPS)
    start(x_r_)

    @pl.loop(0, tiles)
    def _(i):
        f_out[pl.ds(pl.multiple_of(i * TILE, TILE), TILE), :] = apply_tile(i, oc).astype(BF16)
        f_copy(i).start()

    @pl.loop(0, tiles)
    def _(i):
        at = pl.ds(pl.multiple_of(i * TILE, TILE), TILE)
        f = apply_tile(i, c)
        branch[at, :] = f
        sq[:, at] = flat(f)

    x_r_.wait_recv()
    x_g.wait_recv()
    for j, (w, out) in enumerate(zip(weights, (o1, o3, o2))):
        out[c] = own[j, c] * ratio_out[j:j + 1]
        out[oc] = (w[oc] + g_in[j]) * ratio_in[j:j + 1]

    @pl.loop(0, tiles)
    def _(i):
        at = pl.ds(pl.multiple_of(i * TILE, TILE), TILE)
        f_copy(i).wait_recv()
        sq[:, at] = sq[:, at] + flat(f_in[at, :].astype(F32))

    mine = []
    for d in range(1, hn):
        copy = pltpu.make_async_remote_copy(
            src_ref=sq, dst_ref=sq_in.at[d - 1],
            send_sem=sq_s.at[d - 1], recv_sem=sq_r.at[d - 1],
            device_id={"head": lax.rem(hme + d, hn)}, device_id_type=MESH,
        )
        copy.start()
        mine.append(copy)
    for copy, when in pending:
        if when is None:
            copy.wait_send()
        else:
            pl.when(when)(copy.wait_send)

    @pl.loop(0, tiles)
    def _(i):
        f_copy(i).wait_send()

    x_a.wait_recv()
    total = sq[...]
    for d, copy in enumerate(mine):
        copy.wait_recv()
        total = total + sq_in[d]
    for copy in mine:
        copy.wait_send()
    sq[...] = lax.rsqrt(total * (1.0 / (hn * width)) + EPS)

    @pl.loop(0, tiles)
    def _(i):
        at = pl.ds(pl.multiple_of(i * TILE, TILE), TILE)
        inv = column(sq[0:1, at])[:, :1]
        mixed[at, lanes(c)] = (attn[at, :] + branch[at, :] * inv * gain[:, lanes(c)]).astype(BF16)
        other = f_in[at, :].astype(F32) * inv * gain[:, lanes(oc)]
        mixed[at, lanes(oc)] = (attn_in[at, :].astype(F32) + other).astype(BF16)


def local(n, hn, queries, keys, values, rate, fast_gate, fast_up, fast_down, out_gain):
    rows, width = queries.shape
    heads, shard, hd = fast_gate.shape
    line = n // 2
    piece = (3, shard, hd)
    dma = pltpu.SemaphoreType.DMA
    vmem = pl.BlockSpec(memory_space=pltpu.VMEM)
    return pl.pallas_call(
        functools.partial(kernel, n, hn),
        out_shape=(
            jax.ShapeDtypeStruct((rows, width), BF16),
            jax.ShapeDtypeStruct(fast_gate.shape, F32),
            jax.ShapeDtypeStruct(fast_up.shape, F32),
            jax.ShapeDtypeStruct(fast_down.shape, F32),
        ),
        in_specs=[vmem] * 8,
        out_specs=(vmem,) * 4,
        scratch_shapes=[
            pltpu.VMEM((3, line, 2, shard, hd), BF16),
            pltpu.VMEM((3, line, 2, shard, hd), BF16),
            pltpu.VMEM((3, line, 2, shard, hd), F32),
            pltpu.VMEM((2, 3, line - 1, 2, shard, hd), BF16),
            pltpu.VMEM((2, 3, line - 1, 2, shard, hd), BF16),
            pltpu.VMEM(piece, BF16),
            pltpu.VMEM(piece, F32),
            pltpu.VMEM(piece, F32),
            pltpu.VMEM((3, 2, shard, hd), F32),
            pltpu.VMEM(piece, F32),
            pltpu.VMEM(piece, F32),
            pltpu.VMEM((8, hd), F32),
            pltpu.VMEM((8, hd), F32),
            pltpu.VMEM((2 * rows, hd), BF16),
            pltpu.VMEM((WINDOW + 2 * rows, hd), BF16),
            pltpu.VMEM((WINDOW + 2 * rows, hd), BF16),
            pltpu.VMEM((2,) + rate.shape, F32),
            pltpu.VMEM((2 * rows, hd), BF16),
            pltpu.VMEM((2 * rows, hd), BF16),
            pltpu.VMEM((2, 2 * rows, hd), BF16),
            pltpu.VMEM((rows, hd), F32),
            pltpu.VMEM((rows, hd), BF16),
            pltpu.VMEM((rows, hd), BF16),
            pltpu.VMEM((rows, hd), F32),
            pltpu.VMEM((rows, hd), BF16),
            pltpu.VMEM((rows, hd), BF16),
            pltpu.VMEM((8, rows), F32),
            pltpu.VMEM((hn - 1, 8, rows), F32),
        ]
        + [dma((2, 3, line - 1))] * 6
        + [dma((9,))] * 2
        + [dma((2,))] * 2
        + [dma((rows // TILE,))] * 2
        + [dma((hn - 1,))] * 2,
        compiler_params=pltpu.CompilerParams(
            collective_id=0, has_side_effects=True, vmem_limit_bytes=60 * 1024 * 1024
        ),
        name="ttt_layer",
    )(queries, keys, values, rate, out_gain.reshape(1, width), fast_gate, fast_up, fast_down)


def solution(mesh):
    weights = P("head", "seq", None)
    tokens = P("seq", "head")
    return jax.shard_map(
        functools.partial(local, mesh.shape["seq"], mesh.shape["head"]),
        mesh=mesh,
        in_specs=(tokens, tokens, tokens, P("head", "seq"), weights, weights, weights, P("head")),
        out_specs=(tokens, weights, weights, weights),
        check_vma=False,
    )
```

profile of v0, /device:TPU:0, one launch (start us, length us, event | category | flops | bytes accessed | tf_op | source)
XLA Modules:
  0.0 126.0 jit_solution(8546172419968905860)
XLA Ops:
  0.6 120.2 %ttt_layer.1 = (bf16[512,1024]{1,0:T(8,128)(2,1)}, f32[2,64,512]{2,1,0:T(8,128)}, f32[2,64,512]{2,1,0:T(8,128)}, f32[2,64,512]{2,1,0:T(8,128)}) custom-call(bf16[512,1024]{1,0:T(8,128)(2,1)} %q.1, bf16[512,1024]{1,0:T(8,128)(2,1)} %k.1, bf16[512,1024]{1,0:T(8,128)(2,1)} %v.1, f32[2,512]{1,0:T(2,128)} %rate.1, f32[1,1024]{1,0:T(1,128)} %bitcast.1, ...), custom_call_target="tpu_custom_call" | custom-call | tf_op jit(solution)/shard_map/ttt_layer/pallas_call | solution.py:401
  120.9 0.0 copy-start.2
  120.9 2.3 %copy.16 = bf16[512,1024]{1,0:T(8,128)(2,1)} copy(bf16[512,1024]{1,0:T(8,128)(2,1)} %get-tuple-element.8) | data formatting | bytes 2097152
  123.2 0.0 copy-done.2
  123.2 0.0 copy-start.1
  123.2 0.7 copy.17
  123.9 0.3 copy-done.1
  124.2 0.0 copy-start
  124.2 0.7 copy.18
  124.9 0.3 copy-done
  125.3 0.7 copy.19
Async XLA Ops:
  120.9 2.3 %copy-start.2 = (f32[2,64,512]{2,1,0:T(8,128)S(1)}, f32[2,64,512]{2,1,0:T(8,128)}, u32[]{:S(2)}) copy-start(f32[2,64,512]{2,1,0:T(8,128)} %get-tuple-element.9) | copy-start | bytes 786436
  123.2 1.0 copy-start.1
  124.2 1.0 copy-start
where the time goes:
time: 126 us
  Pallas kernels  120 us (95%)
  local copies, waits for them, and re-layouts  5.1 us (4%)
    pallas_call x1, Pallas kernels, local(): pl.pallas_call(functools.partial(kernel, n, hn), out_shape=(jax.ShapeDtyp...  120 us
    unnamed x10, local copies, waits for them, and re-layouts  5.1 us

commit v1 on v0

v1 whole, which is shorter than its diff:
```python
import functools
import math

import jax
import jax.numpy as jnp
from jax import lax
from jax.experimental import pallas as pl
from jax.experimental.pallas import tpu as pltpu
from jax.sharding import PartitionSpec as P

WINDOW = 512
EPS = 1e-06
TILE = 128
WIDE = 256
LAG = 3
FIRST = 1
PARTS = 4
NONE = -1e30
MESH = pl.DeviceIdType.MESH
F32 = jnp.float32
BF16 = jnp.bfloat16
scope = jax.named_scope


def dot(a, b):
    return jnp.dot(a, b, preferred_element_type=F32)


def dot_lhs_t(a, b):
    return lax.dot_general(a, b, (((0,), (0,)), ((), ())), preferred_element_type=F32)


def dot_rhs_t(a, b):
    return lax.dot_general(a, b, (((1,), (1,)), ((), ())), preferred_element_type=F32)


def kernel(
    n, hn,
    q, k, v, rate, gain, w1, w3, w2,
    mixed, o1, o3, o2,
    w_in, rate_in, gain_in, wg, ug, pg, sum_out, sum_in, sum_x, wb_out, g_in,
    ratio_out, ratio_in, qx, kx, vx, kt, eta_x, gv, hid, dab, pre, attn,
    attn_out, attn_in, h2, branch, f_out, f_in, sq, sq_in,
    ag_s, ag_r, in_s, in_r, ex_s, ex_r, ou_s, ou_r, l_s, x_s, x_r, v_s, v_r, halo_s, halo_r,
    g_s, g_r, a_s, a_r, f_s, f_r, sq_s, sq_r,
):
    rows, width = q.shape
    heads, shard, hd = w1.shape
    half = hd // 2
    line = n // 2
    tiles = rows // TILE
    me = lax.axis_index("seq")
    hme = lax.axis_index("head")
    m = lax.div(me, 2)
    c = lax.rem(me, 2)
    oc = 1 - c
    partner = 2 * m + oc
    step_to = (1, -1)
    chunks = [(0, 0), (1, 0), (0, 1), (1, 1), (2, 0), (2, 1)]
    middle = line // 2
    parts = math.gcd(PARTS, line)
    deep = line // parts
    left = m < middle
    inward = jnp.where(left, 1, -1)
    edge = jnp.where(left, m, line - 1 - m)
    inner = edge == middle - 1

    def seq_at(b):
        return 2 * lax.rem(b + line, line) + c

    def lanes(i):
        return pl.ds(pl.multiple_of(i * hd, hd), hd)

    def block(i):
        return pl.ds(pl.multiple_of(i * rows, rows), rows)

    def after_pad(i):
        return pl.ds(pl.multiple_of(WINDOW + i * rows, TILE), rows)

    def tile_at(i):
        return pl.ds(pl.multiple_of(i * TILE, TILE), TILE)

    def halves(h):
        return slice(h * half, (h + 1) * half)

    barrier = pltpu.get_barrier_semaphore()
    for s in (partner, seq_at(m + 1), seq_at(m - 1)):
        pl.semaphore_signal(barrier, inc=1, device_id={"seq": s}, device_id_type=MESH)
    for d in range(1, hn):
        peer = lax.rem(hme + d, hn)
        for s in (me, partner):
            pl.semaphore_signal(
                barrier, inc=1, device_id={"seq": s, "head": peer}, device_id_type=MESH
            )

    loads = [
        pltpu.make_async_copy(src, dst, l_s.at[i])
        for i, (src, dst) in enumerate(
            (
                (w1, w_in.at[0]), (w3, w_in.at[1]), (w2, w_in.at[2]),
                (k.at[:, lanes(c)], kx.at[after_pad(c)]),
                (v.at[:, lanes(c)], vx.at[after_pad(c)]),
                (q.at[:, lanes(c)], qx.at[block(c)]),
                (rate, rate_in), (gain, gain_in),
            )
        )
    ]
    for copy in loads:
        copy.start()
    with scope("a_load"):
        for j in range(3):
            loads[j].wait()
            wg[j, m, c] = w_in[j, c].astype(BF16)
            wb_out[j] = w_in[j, oc].astype(BF16)
    with scope("a_barrier"):
        pl.semaphore_wait(barrier, 3 + 2 * (hn - 1))

    pending = []

    def start(copy, when=None):
        if when is None:
            copy.start()
        else:
            pl.when(when)(copy.start)
        pending.append((copy, when))

    def wait(copy, when):
        pl.when(when)(copy.wait_recv)

    def remote(src, dst, ss, rr, **where):
        return pltpu.make_async_remote_copy(
            src_ref=src, dst_ref=dst, send_sem=ss, recv_sem=rr,
            device_id=where, device_id_type=MESH,
        )

    def to_partner(i, src, dst):
        return remote(src, dst, x_s.at[i], x_r.at[i], seq=partner)

    x_w = to_partner(0, wb_out, wg.at[:, m, c])
    x_k = to_partner(1, k.at[:, lanes(oc)], kx.at[after_pad(c)])
    x_e = to_partner(2, rate, eta_x)
    x_q = to_partner(3, q.at[:, lanes(oc)], qx.at[block(c)])
    x_n = to_partner(4, ratio_out, ratio_in)
    x_v = [
        remote(
            v.at[i * TILE:(i + 1) * TILE, lanes(oc)],
            vx.at[pl.ds(pl.multiple_of(WINDOW + c * rows + i * TILE, TILE), TILE)],
            v_s.at[i], v_r.at[i], seq=partner,
        )
        for i in range(tiles)
    ]
    x_g = [
        remote(ug.at[i, m, oc], g_in.at[i], g_s.at[i], g_r.at[i], seq=partner) for i in range(6)
    ]
    has_next = m < line - 1
    has_prev = m > 0

    def halo(x, first, count, i):
        return remote(
            x.at[2 * rows + first:2 * rows + first + count], x.at[first:first + count],
            halo_s.at[i], halo_r.at[i], seq=seq_at(m + 1),
        )

    halo_k = halo(kx, 0, WINDOW, 0)
    halo_v = [halo(vx, i * TILE, TILE, 1 + i) for i in range(WINDOW // TILE)]

    def link(ss, rr, src, dst, d, i, s):
        return remote(
            src, dst, ss.at[d, i, s - 1], rr.at[d, i, s - 1], seq=seq_at(m + step_to[d])
        )

    def ahead(d):
        return line - 1 - m if d == 0 else m

    def w_piece(i, b):
        return wg.at[i % 3, b, c if i < 3 else oc]

    def gather_copy(i, d, s):
        b = lax.rem(m - step_to[d] * (s - 1) + line, line)
        return link(ag_s, ag_r, w_piece(i, b), w_piece(i, b), d, i, s)

    def gather_arrived(i, d, s, passing):
        b = lax.rem(m - step_to[d] * s + line, line)
        onward = ahead(d) >= 1 if passing else ahead(d) == 0
        wait(
            link(ag_s, ag_r, w_piece(i, b), w_piece(i, b), d, i, s),
            jnp.logical_and(ahead(1 - d) >= s, onward),
        )

    def gather_send(i, s):
        for d in range(2):
            if s > 1:
                gather_arrived(i, d, s - 1, True)
            start(
                gather_copy(i, d, s),
                jnp.logical_and(ahead(d) >= 1, ahead(1 - d) >= s - 1),
            )

    def gather_finish(i):
        for d in range(2):
            for s in range(1, line):
                gather_arrived(i, d, s, False)

    def part(r):
        return slice(r * deep, (r + 1) * deep)

    def inward_copy(i, r, across):
        return remote(
            sum_out.at[i, part(r)], (sum_x if across else sum_in).at[i, part(r)],
            (ex_s if across else in_s).at[i, r], (ex_r if across else in_r).at[i, r],
            seq=seq_at(m + inward),
        )

    def outward_copy(i, r):
        piece = ug.at[i, part(r)]
        return remote(piece, piece, ou_s.at[i, r], ou_r.at[i, r], seq=seq_at(m - inward))

    def sum_first(i, r):
        @pl.when(edge == 0)
        def _():
            sum_out[i, part(r)] = pg[i, part(r)].astype(BF16)

        start(inward_copy(i, r, False), jnp.logical_and(edge == 0, jnp.logical_not(inner)))
        start(inward_copy(i, r, True), jnp.logical_and(edge == 0, inner))

    def sum_on(i, r):
        @pl.when(edge > 0)
        def _():
            inward_copy(i, r, False).wait_recv()
            total = pg[i, part(r)] + sum_in[i, part(r)].astype(F32)
            pg[i, part(r)] = total
            sum_out[i, part(r)] = total.astype(BF16)

        start(inward_copy(i, r, False), jnp.logical_and(edge > 0, jnp.logical_not(inner)))
        start(inward_copy(i, r, True), jnp.logical_and(edge > 0, inner))

    def sum_back(i, r):
        j, h = chunks[i]

        @pl.when(inner)
        def _():
            inward_copy(i, r, True).wait_recv()
            total = pg[i, part(r)] + sum_x[i, part(r)].astype(F32)
            ug[i, part(r)] = (total + wg[j, part(r), :, :, halves(h)].astype(F32)).astype(BF16)

        wait(outward_copy(i, r), jnp.logical_not(inner))
        start(outward_copy(i, r), edge > 0)

    def column(row):
        return jnp.transpose(jnp.broadcast_to(row, (TILE, row.shape[1])))

    def as_row(col):
        return jnp.transpose(jnp.broadcast_to(col, (TILE, TILE)))[:8]

    def w_cols(j, h):
        return wg[j, :, :, :, halves(h)].reshape(n * shard, half)

    def w_rows(j, h):
        return wg[j].reshape(n * shard, hd)[halves(h)]

    def u_all(i):
        return ug[i].reshape(n * shard, half)

    def forward(b):
        for h in range(2):

            @pl.loop(0, rows // WIDE)
            def _(i):
                at = pl.ds(pl.multiple_of(b * rows + i * WIDE, WIDE), WIDE)
                kt = kx[pl.ds(pl.multiple_of(WINDOW + b * rows + i * WIDE, WIDE), WIDE), :]
                a = dot(kt, w_cols(0, h))
                up = dot(kt, w_cols(1, h))
                g = jax.nn.sigmoid(a)
                ag = a * g
                hid[at, halves(h)] = (ag * up).astype(BF16)
                pre[0, at, halves(h)] = up * g * (1.0 + a * (1.0 - g))
                pre[1, at, halves(h)] = ag

    def scaled_values(b):
        eta = column((rate_in if b is c else eta_x)[pl.ds(c, 1), :])[:, :1]
        vb = vx[after_pad(b), :]
        gv[block(b), :] = (eta * vb.astype(F32)).astype(BF16)

    def backward(b, h):
        @pl.loop(0, rows // WIDE)
        def _(i):
            at = pl.ds(pl.multiple_of(b * rows + i * WIDE, WIDE), WIDE)
            back = dot_rhs_t(gv[at, :], w_rows(2, h))
            dab[0, at, halves(h)] = (back * pre[0, at, halves(h)]).astype(BF16)
            dab[1, at, halves(h)] = (back * pre[1, at, halves(h)]).astype(BF16)

    def product(i):
        j, h = chunks[i]
        if j == 2:
            g = dot_lhs_t(hid[...], gv[:, halves(h)])
        else:
            g = dot(kt[...], dab[j, :, halves(h)])
        pg[i] = g.reshape(line, 2, shard, half)

    def softmax(s, ok):
        s = jnp.where(ok, s * (1.0 / math.sqrt(hd)), NONE)
        top = jnp.max(s, axis=1, keepdims=True)
        e = jnp.exp(s - top)
        total = jnp.sum(e, axis=1, keepdims=True)
        return (e * (1.0 / total)).astype(BF16)

    def local_attention(b, i):
        span = WINDOW + TILE
        base = pl.multiple_of(b * rows + i * TILE, TILE)
        s = dot_rhs_t(qx[pl.ds(base, TILE), :], kx[pl.ds(base, span), :])
        r = lax.broadcasted_iota(jnp.int32, (TILE, span), 0)
        u = lax.broadcasted_iota(jnp.int32, (TILE, span), 1)
        ok = (u > r) & (u <= r + WINDOW) & (base + u + m * 2 * rows >= WINDOW)
        p = softmax(s, ok)
        attn[b, tile_at(i), :] = dot(p, vx[pl.ds(base, span), :])

    def attn_to(i):
        at = slice(i * TILE, (i + 1) * TILE)
        return remote(attn_out.at[at], attn_in.at[at], a_s.at[i], a_r.at[i], seq=partner)

    def attention_out(i):
        attn_out[i * TILE:(i + 1) * TILE, :] = attn[oc, i * TILE:(i + 1) * TILE, :].astype(BF16)
        start(attn_to(i))

    def squares(x):
        x = x.astype(F32)
        return jnp.sum(x * x, axis=0, keepdims=True)

    def set_ratio(i):
        j, h = chunks[i]
        old = ratio_out[j:j + 1, halves(h)]
        ratio_out[j:j + 1, halves(h)] = old / jnp.sqrt(squares(u_all(i)) + EPS)

    def hidden_two(h, i):
        at = slice(i * WIDE, (i + 1) * WIDE)
        a = dot(qx[at, :], u_all(2 * h)) * ratio_out[0:1, halves(h)]
        g = dot(qx[at, :], u_all(2 * h + 1)) * ratio_out[1:2, halves(h)]
        h2[at, halves(h)] = (a * jax.nn.sigmoid(a) * g).astype(BF16)

    def f_copy(i, h):
        at = tile_at(i)
        return remote(
            f_out.at[at, halves(h)], f_in.at[at, halves(h)],
            f_s.at[h, i], f_r.at[h, i], seq=partner,
        )

    def apply_tile(b, i, h):
        ht = h2[pl.ds(pl.multiple_of(b * rows + i * TILE, TILE), TILE), :]
        f = dot(ht, u_all(4 + h)) * ratio_out[2:3, halves(h)]
        part = as_row(jnp.sum(f * f, axis=1, keepdims=True))
        where = 0 if b is c else 1
        if h == 0:
            sq[where, :, tile_at(i)] = part
        else:
            sq[where, :, tile_at(i)] = sq[where, :, tile_at(i)] + part
        return f

    def apply_out(h):
        @pl.loop(0, tiles)
        def _(i):
            f_out[tile_at(i), halves(h)] = apply_tile(oc, i, h).astype(BF16)
            f_copy(i, h).start()

    def apply_own(h):
        @pl.loop(0, tiles)
        def _(i):
            branch[tile_at(i), halves(h)] = apply_tile(c, i, h)

    start(x_w)
    start(x_k)
    start(x_e)
    for copy in x_v:
        start(copy)
    start(x_q)
    for j in range(3):
        gather_send(j, 1)

    @pl.when(m == 0)
    def _():
        for x in (kx, vx):
            x[:WINDOW, :] = jnp.zeros((WINDOW, hd), BF16)

    for copy in loads[3:]:
        copy.wait()
    with scope("b_xw"):
        x_w.wait_recv()
    for j in range(3):
        gather_send(3 + j, 1)
    local_early = jnp.logical_and(jnp.logical_and(c == 1, m == 0), has_next)
    local_late = jnp.logical_and(jnp.logical_and(c == 1, m > 0), has_next)
    passed = jnp.logical_and(c == 0, has_next)
    for copy in [halo_k] + halo_v:
        start(copy, local_early)
    with scope("b_relay"):
        for s in range(2, line):
            for j in range(3):
                gather_send(j, s)
                gather_send(3 + j, s)
    for copy in [halo_k] + halo_v:
        start(copy, local_late)
    with scope("b_xk"):
        x_k.wait_recv()
    start(halo_k, passed)
    with scope("b_kt"):
        kt[...] = jnp.transpose(kx[WINDOW:, :])
    with scope("b_w13"):
        for j in range(2):
            gather_finish(j)
            gather_finish(3 + j)
    with scope("b_fwd_own"):
        forward(c)
    with scope("b_fwd_oc"):
        forward(oc)
    scaled_values(c)
    for j in range(2):
        ratio_out[j:j + 1] = jnp.sqrt(squares(wg[j].reshape(n * shard, hd)))
    with scope("b_w2"):
        gather_finish(2)
        gather_finish(5)
    with scope("b_bwd_own"):
        for h in range(2):
            backward(c, h)
        ratio_out[2:3] = jnp.sqrt(squares(wg[2].reshape(n * shard, hd)))
    with scope("b_xv"):
        x_e.wait_recv()
        for i in range(tiles):
            x_v[i].wait_recv()
            start(halo_v[i], passed)
    with scope("b_bwd_oc"):
        scaled_values(oc)
        for h in range(2):
            backward(oc, h)

    with scope("prods"):
        for i in range(6):
            product(i)
            for r in range(parts):
                sum_first(i, r)

    def halo_wait():
        for copy in [halo_k] + halo_v:
            wait(copy, has_prev)

    tasks = (
        [lambda: pl.when(c == 0)(x_q.wait_recv)]
        + [lambda i=i: local_attention(1, i) for i in range(tiles)]
        + [lambda: pl.when(c == 1)(x_q.wait_recv), halo_wait]
        + [lambda i=i: local_attention(0, i) for i in range(tiles)]
        + [lambda i=i: attention_out(i) for i in range(tiles)]
    )
    done = []

    def task():
        if tasks:
            with scope("task%d" % len(done)):
                tasks.pop(0)()
            done.append(0)

    def finished(i):
        set_ratio(i)
        start(x_g[i])
        if i == 1 or i == 3:
            for b in range(2 * rows // WIDE):
                tasks.append(lambda b=b: hidden_two(i // 2, b))

    pieces = [(i, r) for i in range(6) for r in range(parts)]
    for p in range(len(pieces) + LAG):
        with scope("p%d" % p):
            if p < len(pieces):
                sum_on(*pieces[p])
            if p >= LAG:
                sum_back(*pieces[p - LAG])
        if p >= LAG:
            i, r = pieces[p - LAG]
            if r == parts - 1:
                finished(i)
            if i == 4 and r == parts - 1:
                while tasks:
                    task()
                with scope("apply0"):
                    apply_out(0)
                    apply_own(0)
        if p >= FIRST:
            task()

    with scope("t_out"):
        start(x_n)
        apply_out(1)
    mine = []
    for d in range(hn):
        slot = hn - 1 + d
        mine.append(
            remote(
                sq.at[1], sq_in.at[slot], sq_s.at[slot], sq_r.at[slot],
                seq=partner, head=lax.rem(hme + d, hn),
            )
        )
    for copy in mine:
        copy.start()
    with scope("t_own"):
        apply_own(1)
    for d in range(1, hn):
        copy = remote(
            sq.at[0], sq_in.at[d - 1], sq_s.at[d - 1], sq_r.at[d - 1],
            head=lax.rem(hme + d, hn),
        )
        copy.start()
        mine.append(copy)
    with scope("t_outs"):
        x_n.wait_recv()
        for copy in x_g:
            copy.wait_recv()
        for i, (j, h) in enumerate(chunks):
            out = (o1, o3, o2)[j]
            at = halves(h)
            out[c, :, at] = ug[i, m, c].astype(F32) * ratio_out[j:j + 1, at]
            out[oc, :, at] = g_in[i].astype(F32) * ratio_in[j:j + 1, at]
    with scope("t_sends"):
        for copy, when in pending:
            if when is None:
                copy.wait_send()
            else:
                pl.when(when)(copy.wait_send)
    with scope("t_sq"):
        total = sq[0]
        for copy in mine:
            copy.wait_recv()
        for slot in range(2 * hn - 1):
            total = total + sq_in[slot]
        for copy in mine:
            copy.wait_send()
        sq[0] = lax.rsqrt(total * (1.0 / (hn * width)) + EPS)

    with scope("t_mix_own"):

        @pl.loop(0, tiles)
        def _(i):
            at = tile_at(i)
            inv = column(sq[0, 0:1, at])[:, :1]
            own_part = branch[at, :] * inv * gain_in[:, lanes(c)]
            mixed[at, lanes(c)] = (attn[c, at, :] + own_part).astype(BF16)

    with scope("t_mix_oc"):
        for i in range(tiles):
            attn_to(i).wait_recv()

        @pl.loop(0, tiles)
        def _(i):
            at = tile_at(i)
            for h in range(2):
                f_copy(i, h).wait_recv()
                f_copy(i, h).wait_send()
            inv = column(sq[0, 0:1, at])[:, :1]
            other = f_in[at, :].astype(F32) * inv * gain_in[:, lanes(oc)]
            mixed[at, lanes(oc)] = (attn_in[at, :].astype(F32) + other).astype(BF16)


def local(n, hn, queries, keys, values, rate, fast_gate, fast_up, fast_down, out_gain):
    rows, width = queries.shape
    heads, shard, hd = fast_gate.shape
    line = n // 2
    half = hd // 2
    tiles = rows // TILE
    sums = (6, line, 2, shard, half)
    dma = pltpu.SemaphoreType.DMA
    vmem = pl.BlockSpec(memory_space=pltpu.VMEM)
    hbm = pl.BlockSpec(memory_space=pltpu.HBM)
    return pl.pallas_call(
        functools.partial(kernel, n, hn),
        out_shape=(
            jax.ShapeDtypeStruct((rows, width), BF16),
            jax.ShapeDtypeStruct(fast_gate.shape, F32),
            jax.ShapeDtypeStruct(fast_up.shape, F32),
            jax.ShapeDtypeStruct(fast_down.shape, F32),
        ),
        in_specs=[hbm] * 8,
        out_specs=(vmem,) * 4,
        scratch_shapes=[
            pltpu.VMEM((3, 2, shard, hd), F32),
            pltpu.VMEM(rate.shape, F32),
            pltpu.VMEM((1, width), F32),
            pltpu.VMEM((3, line, 2, shard, hd), BF16),
            pltpu.VMEM(sums, BF16),
            pltpu.VMEM(sums, F32),
            pltpu.VMEM(sums, BF16),
            pltpu.VMEM(sums, BF16),
            pltpu.VMEM(sums, BF16),
            pltpu.VMEM((3, shard, hd), BF16),
            pltpu.VMEM((6, shard, half), BF16),
            pltpu.VMEM((8, hd), F32),
            pltpu.VMEM((8, hd), F32),
            pltpu.VMEM((2 * rows, hd), BF16),
            pltpu.VMEM((WINDOW + 2 * rows, hd), BF16),
            pltpu.VMEM((WINDOW + 2 * rows, hd), BF16),
            pltpu.VMEM((hd, 2 * rows), BF16),
            pltpu.VMEM(rate.shape, F32),
            pltpu.VMEM((2 * rows, hd), BF16),
            pltpu.VMEM((2 * rows, hd), BF16),
            pltpu.VMEM((2, 2 * rows, hd), BF16),
            pltpu.VMEM((2, 2 * rows, hd), F32),
            pltpu.VMEM((2, rows, hd), F32),
            pltpu.VMEM((rows, hd), BF16),
            pltpu.VMEM((rows, hd), BF16),
            pltpu.VMEM((2 * rows, hd), BF16),
            pltpu.VMEM((rows, hd), F32),
            pltpu.VMEM((rows, hd), BF16),
            pltpu.VMEM((rows, hd), BF16),
            pltpu.VMEM((2, 8, rows), F32),
            pltpu.VMEM((2 * hn - 1, 8, rows), F32),
        ]
        + [dma((2, 6, line - 1))] * 2
        + [dma((6, math.gcd(PARTS, line)))] * 6
        + [dma((8,))]
        + [dma((5,))] * 2
        + [dma((tiles,))] * 2
        + [dma((1 + WINDOW // TILE,))] * 2
        + [dma((6,))] * 2
        + [dma((tiles,))] * 2
        + [dma((2, tiles))] * 2
        + [dma((2 * hn - 1,))] * 2,
        compiler_params=pltpu.CompilerParams(
            collective_id=0, has_side_effects=True, vmem_limit_bytes=60 * 1024 * 1024
        ),
        name="ttt_layer",
    )(queries, keys, values, rate, out_gain.reshape(1, width), fast_gate, fast_up, fast_down)


def solution(mesh):
    weights = P("head", "seq", None)
    tokens = P("seq", "head")
    return jax.shard_map(
        functools.partial(local, mesh.shape["seq"], mesh.shape["head"]),
        mesh=mesh,
        in_specs=(tokens, tokens, tokens, P("head", "seq"), weights, weights, weights, P("head")),
        out_specs=(tokens, weights, weights, weights),
        check_vma=False,
    )
```

time: 126 us -> 109 us (0.87)
  Pallas kernels: 120 us -> 102 us
    pallas_call x1, Pallas kernels: 120 us -> 102 us  [local(): pl.pallas_call(functools.partial(kernel, n, hn), out_shape=(jax.ShapeDtyp...]
where the time goes in v1:
time: 109 us; the launch traced here: 108 us
  Pallas kernels  102 us (94%)
  local copies, waits for them, and re-layouts  5.1 us (5%)
    pallas_call x1, Pallas kernels, local(): pl.pallas_call(functools.partial(kernel, n, hn), out_shape=(jax.ShapeDtyp...  102 us
    unnamed x10, local copies, waits for them, and re-layouts  5.1 us

profile of v1, /device:TPU:0, one launch (start us, length us, event | category | flops | bytes accessed | tf_op | source)
XLA Modules:
  0.0 107.7 jit_solution(18377836595920558866)
XLA Ops:
  0.6 102.0 %ttt_layer.1 = (bf16[512,1024]{1,0:T(8,128)(2,1)}, f32[2,64,512]{2,1,0:T(8,128)}, f32[2,64,512]{2,1,0:T(8,128)}, f32[2,64,512]{2,1,0:T(8,128)}) custom-call(bf16[512,1024]{1,0:T(8,128)(2,1)} %q.1, bf16[512,1024]{1,0:T(8,128)(2,1)} %k.1, bf16[512,1024]{1,0:T(8,128)(2,1)} %v.1, f32[2,512]{1,0:T(2,128)} %rate.1, f32[1,1024]{1,0:T(1,128)} %bitcast.1, ...), custom_call_target="tpu_custom_call" | custom-call | tf_op jit(solution)/shard_map/ttt_layer/pallas_call | solution.py:568
  102.6 0.0 copy-start.2
  102.6 2.3 %copy.16 = bf16[512,1024]{1,0:T(8,128)(2,1)} copy(bf16[512,1024]{1,0:T(8,128)(2,1)} %get-tuple-element.8) | data formatting | bytes 2097152
  104.9 0.0 copy-done.2
  104.9 0.0 copy-start.1
  104.9 0.7 copy.17
  105.6 0.3 copy-done.1
  106.0 0.0 copy-start
  106.0 0.7 copy.18
  106.7 0.3 copy-done
  107.0 0.7 copy.19
Async XLA Ops:
  102.6 2.3 %copy-start.2 = (f32[2,64,512]{2,1,0:T(8,128)S(1)}, f32[2,64,512]{2,1,0:T(8,128)}, u32[]{:S(2)}) copy-start(f32[2,64,512]{2,1,0:T(8,128)} %get-tuple-element.9) | copy-start | bytes 786436
  104.9 1.0 copy-start.1
  106.0 1.0 copy-start

commit v2 on v1

v2 whole, which is shorter than its diff:
```python
import functools
import math

import jax
import jax.numpy as jnp
from jax import lax
from jax.experimental import pallas as pl
from jax.experimental.pallas import tpu as pltpu
from jax.sharding import PartitionSpec as P

WINDOW = 512
EPS = 1e-06
TILE = 128
WIDE = 256
LAG = 3
FIRST = 1
PARTS = 4
NONE = -1e30
MESH = pl.DeviceIdType.MESH
F32 = jnp.float32
BF16 = jnp.bfloat16
scope = jax.named_scope


def dot(a, b):
    return jnp.dot(a, b, preferred_element_type=F32)


def dot_lhs_t(a, b):
    return lax.dot_general(a, b, (((0,), (0,)), ((), ())), preferred_element_type=F32)


def dot_rhs_t(a, b):
    return lax.dot_general(a, b, (((1,), (1,)), ((), ())), preferred_element_type=F32)


def kernel(
    n, hn,
    q, k, v, rate, gain, w1, w3, w2,
    mixed_to, o1_to, o3_to, o2_to,
    mixed, o_all, w_in, rate_in, gain_in, wg, ug_a, ug_b, pg_a, pg_b, out_a, out_b, in_a, in_b, ex_a, ex_b, wb_out, gi_a, gi_b,
    ratio_out, ratio_in, qx, kx, vx, kt, eta_x, gv, hid, dab, pre, attn,
    attn_out, attn_in, h2, branch, f_out, f_in, sq, sq_in,
    ag_s, ag_r, in_r, back_r, l_s, x_s, x_r, k_r, v_r, halo_r, one_s, g_r,
):
    rows, width = q.shape
    heads, shard, hd = w1.shape
    half = hd // 2
    line = n // 2
    tiles = rows // TILE
    me = lax.axis_index("seq")
    hme = lax.axis_index("head")
    m = lax.div(me, 2)
    c = lax.rem(me, 2)
    oc = 1 - c
    partner = 2 * m + oc
    step_to = (1, -1)
    quarter = hd // 4
    chunks = [
        (j, slice(h * half, (h + 1) * half)) for h in range(2) for j in range(2)
    ] + [(2, slice(h * quarter, (h + 1) * quarter)) for h in range(4)]
    sends = {
        name: one_s.at[i]
        for i, name in enumerate(
            ("in_a", "in_b", "out_a", "out_b", "k", "v", "hk", "hv", "g_a", "g_b", "a", "ar",
             "f", "fr", "q", "qr", "mixed", "new")
        )
    }
    us, pgs = (ug_a, ug_b), (pg_a, pg_b)
    outs, ins, exs, gis = (out_a, out_b), (in_a, in_b), (ex_a, ex_b), (gi_a, gi_b)
    middle = line // 2

    def parts(i):
        return math.gcd(PARTS if i < 4 else PARTS // 2, line)

    def chunk(bufs, i):
        return bufs[0].at[i] if i < 4 else bufs[1].at[i - 4]

    def part(bufs, i, r):
        deep = line // parts(i)
        return chunk(bufs, i).at[r * deep:(r + 1) * deep]

    left = m < middle
    inward = jnp.where(left, 1, -1)
    edge = jnp.where(left, m, line - 1 - m)
    inner = edge == middle - 1

    def seq_at(b):
        return 2 * lax.rem(b + line, line) + c

    def lanes(i):
        return pl.ds(pl.multiple_of(i * hd, hd), hd)

    def block(i):
        return pl.ds(pl.multiple_of(i * rows, rows), rows)

    def after_pad(i):
        return pl.ds(pl.multiple_of(WINDOW + i * rows, TILE), rows)

    def tile_at(i):
        return pl.ds(pl.multiple_of(i * TILE, TILE), TILE)

    def halves(h):
        return slice(h * half, (h + 1) * half)

    barrier = pltpu.get_barrier_semaphore()
    for s in (partner, seq_at(m + 1), seq_at(m - 1)):
        pl.semaphore_signal(barrier, inc=1, device_id={"seq": s}, device_id_type=MESH)
    for d in range(1, hn):
        peer = lax.rem(hme + d, hn)
        for s in (me, partner):
            pl.semaphore_signal(
                barrier, inc=1, device_id={"seq": s, "head": peer}, device_id_type=MESH
            )

    loads = [
        pltpu.make_async_copy(src, dst, l_s.at[i])
        for i, (src, dst) in enumerate(
            (
                (w1, w_in.at[0]), (w3, w_in.at[1]), (w2, w_in.at[2]),
                (k.at[:, lanes(c)], kx.at[after_pad(c)]),
                (v.at[:, lanes(c)], vx.at[after_pad(c)]),
                (q.at[:, lanes(c)], qx.at[block(c)]),
                (rate, rate_in), (gain, gain_in),
            )
        )
    ]
    for copy in loads:
        copy.start()
    with scope("a_load"):
        for j in range(3):
            loads[j].wait()
            wg[j, m, c] = w_in[j, c].astype(BF16)
            wb_out[j] = w_in[j, oc].astype(BF16)
    with scope("a_barrier"):
        pl.semaphore_wait(barrier, 3 + 2 * (hn - 1))

    pending = []

    def start(copy, when=None, alone=True):
        if when is None:
            copy.start()
        else:
            pl.when(when)(copy.start)
        if alone:
            pending.append((copy, when))

    def wait(copy, when):
        pl.when(when)(copy.wait_recv)

    def remote(src, dst, ss, rr, **where):
        return pltpu.make_async_remote_copy(
            src_ref=src, dst_ref=dst, send_sem=ss, recv_sem=rr,
            device_id=where, device_id_type=MESH,
        )

    def group(ref, ss, rr):
        return remote(ref, ref, ss, rr, seq=partner)

    def to_partner(i, src, dst):
        return remote(src, dst, x_s.at[i], x_r.at[i], seq=partner)

    x_w = to_partner(0, wb_out, wg.at[:, m, c])
    def token_copies(src, dst, name, rr):
        return [
            remote(
                src.at[i * TILE:(i + 1) * TILE, lanes(oc)],
                dst.at[pl.ds(pl.multiple_of(WINDOW + c * rows + i * TILE, TILE), TILE)],
                sends[name], rr.at[i], seq=partner,
            )
            for i in range(tiles)
        ]

    x_k = token_copies(k, kx, "k", k_r)
    x_v = token_copies(v, vx, "v", v_r)
    x_e = to_partner(1, rate, eta_x)
    x_q = to_partner(2, q.at[:, lanes(oc)], qx.at[block(c)])
    x_n = to_partner(3, ratio_out, ratio_in)
    x_g = [
        remote(
            chunk(us, i).at[m, oc], chunk(gis, i), sends["g_a" if i < 4 else "g_b"],
            g_r.at[0 if i < 4 else 1], seq=partner,
        )
        for i in range(8)
    ]
    has_next = m < line - 1
    has_prev = m > 0

    def halo(x, i, base):
        return remote(
            x.at[2 * rows + i * TILE:2 * rows + (i + 1) * TILE],
            x.at[i * TILE:(i + 1) * TILE],
            sends["hv" if base else "hk"], halo_r.at[base + i], seq=seq_at(m + 1),
        )

    halo_k = [halo(kx, i, 0) for i in range(WINDOW // TILE)]
    halo_v = [halo(vx, i, WINDOW // TILE) for i in range(WINDOW // TILE)]

    def link(ss, rr, src, dst, d, i, s):
        return remote(
            src, dst, ss.at[d, s - 1], rr.at[d, i, s - 1], seq=seq_at(m + step_to[d])
        )

    def ahead(d):
        return line - 1 - m if d == 0 else m

    def w_piece(i, b):
        return wg.at[i % 3, b, c if i < 3 else oc]

    def gather_copy(i, d, s):
        b = lax.rem(m - step_to[d] * (s - 1) + line, line)
        return link(ag_s, ag_r, w_piece(i, b), w_piece(i, b), d, i, s)

    def gather_arrived(i, d, s, passing):
        b = lax.rem(m - step_to[d] * s + line, line)
        onward = ahead(d) >= 1 if passing else ahead(d) == 0
        wait(
            link(ag_s, ag_r, w_piece(i, b), w_piece(i, b), d, i, s),
            jnp.logical_and(ahead(1 - d) >= s, onward),
        )

    def gather_send(i, s):
        for d in range(2):
            if s > 1:
                gather_arrived(i, d, s - 1, True)
            start(
                gather_copy(i, d, s),
                jnp.logical_and(ahead(d) >= 1, ahead(1 - d) >= s - 1), False,
            )

    def gather_finish(i):
        for d in range(2):
            for s in range(1, line):
                gather_arrived(i, d, s, False)

    def number(i, r):
        return sum(parts(t) for t in range(i)) + r

    def inward_copy(i, r, across):
        return remote(
            part(outs, i, r), part(exs if across else ins, i, r),
            sends["in_a" if i < 4 else "in_b"], (back_r if across else in_r).at[number(i, r)],
            seq=seq_at(m + inward),
        )

    def outward_copy(i, r):
        piece = part(us, i, r)
        return remote(
            piece, piece, sends["out_a" if i < 4 else "out_b"], back_r.at[number(i, r)],
            seq=seq_at(m - inward),
        )

    def sum_first(i, r):
        @pl.when(edge == 0)
        def _():
            part(outs, i, r)[...] = part(pgs, i, r)[...].astype(BF16)

        start(inward_copy(i, r, False), jnp.logical_and(edge == 0, jnp.logical_not(inner)), False)
        start(inward_copy(i, r, True), jnp.logical_and(edge == 0, inner), False)

    def sum_on(i, r):
        @pl.when(edge > 0)
        def _():
            inward_copy(i, r, False).wait_recv()
            total = part(pgs, i, r)[...] + part(ins, i, r)[...].astype(F32)
            part(pgs, i, r)[...] = total
            part(outs, i, r)[...] = total.astype(BF16)

        start(inward_copy(i, r, False), jnp.logical_and(edge > 0, jnp.logical_not(inner)), False)
        start(inward_copy(i, r, True), jnp.logical_and(edge > 0, inner), False)

    def sum_back(i, r):
        j, cols = chunks[i]
        deep = line // parts(i)

        @pl.when(inner)
        def _():
            inward_copy(i, r, True).wait_recv()
            total = part(pgs, i, r)[...] + part(exs, i, r)[...].astype(F32)
            old = wg[j, r * deep:(r + 1) * deep, :, :, cols].astype(F32)
            part(us, i, r)[...] = (total + old).astype(BF16)

        wait(outward_copy(i, r), jnp.logical_not(inner))
        start(outward_copy(i, r), edge > 0, False)

    def column(row):
        return jnp.transpose(jnp.broadcast_to(row, (TILE, row.shape[1])))

    def as_row(col):
        return jnp.transpose(jnp.broadcast_to(col, (col.shape[0], TILE)))[:8]

    def w_cols(j, h):
        return wg[j, :, :, :, halves(h)].reshape(n * shard, half)

    def w_rows(j, h):
        return wg[j].reshape(n * shard, hd)[halves(h)]

    def u_all(i):
        u = chunk(us, i)[...]
        return u.reshape(n * shard, u.shape[-1])

    def forward(b):
        for h in range(2):

            @pl.loop(0, rows // WIDE)
            def _(i):
                at = pl.ds(pl.multiple_of(b * rows + i * WIDE, WIDE), WIDE)
                kt = kx[pl.ds(pl.multiple_of(WINDOW + b * rows + i * WIDE, WIDE), WIDE), :]
                a = dot(kt, w_cols(0, h))
                up = dot(kt, w_cols(1, h))
                g = jax.nn.sigmoid(a)
                ag = a * g
                hid[at, halves(h)] = (ag * up).astype(BF16)
                pre[0, at, halves(h)] = up * g * (1.0 + a * (1.0 - g))
                pre[1, at, halves(h)] = ag

    def scaled_values(b):
        eta = column((rate_in if b is c else eta_x)[pl.ds(c, 1), :])[:, :1]
        vb = vx[after_pad(b), :]
        gv[block(b), :] = (eta * vb.astype(F32)).astype(BF16)

    def backward(b, h):
        @pl.loop(0, rows // WIDE)
        def _(i):
            at = pl.ds(pl.multiple_of(b * rows + i * WIDE, WIDE), WIDE)
            back = dot_rhs_t(gv[at, :], w_rows(2, h))
            dab[h, at, halves(0)] = (back * pre[0, at, halves(h)]).astype(BF16)
            dab[h, at, halves(1)] = (back * pre[1, at, halves(h)]).astype(BF16)

    def product(h):
        g = dot(kt[...], dab[h]) if h < 2 else dot_lhs_t(hid[...], gv[...])
        for i, at in ((2 * h, 0), (2 * h + 1, half)) if h < 2 else zip(
            range(4, 8), range(0, hd, quarter)
        ):
            dst = chunk(pgs, i)
            dst[...] = g[:, at:at + dst.shape[-1]].reshape(dst.shape)

    def softmax(s, ok):
        s = jnp.where(ok, s * (1.0 / math.sqrt(hd)), NONE)
        top = jnp.max(s, axis=1, keepdims=True)
        e = jnp.exp(s - top)
        total = jnp.sum(e, axis=1, keepdims=True)
        return (e * (1.0 / total)).astype(BF16)

    def local_attention(b, i):
        span = WINDOW + TILE
        base = pl.multiple_of(b * rows + i * TILE, TILE)
        s = dot_rhs_t(qx[pl.ds(base, TILE), :], kx[pl.ds(base, span), :])
        r = lax.broadcasted_iota(jnp.int32, (TILE, span), 0)
        u = lax.broadcasted_iota(jnp.int32, (TILE, span), 1)
        ok = (u > r) & (u <= r + WINDOW) & (base + u + m * 2 * rows >= WINDOW)
        p = softmax(s, ok)
        attn[b, tile_at(i), :] = dot(p, vx[pl.ds(base, span), :])

    def attn_to(i):
        at = slice(i * TILE, (i + 1) * TILE)
        return remote(attn_out.at[at], attn_in.at[at], sends["a"], sends["ar"], seq=partner)

    def attention_out(i):
        attn_out[i * TILE:(i + 1) * TILE, :] = attn[oc, i * TILE:(i + 1) * TILE, :].astype(BF16)
        attn_to(i).start()

    def squares(x):
        x = x.astype(F32)
        return jnp.sum(x * x, axis=0, keepdims=True)

    def set_ratio(i):
        j, cols = chunks[i]
        old = ratio_out[j:j + 1, cols]
        ratio_out[j:j + 1, cols] = old / jnp.sqrt(squares(u_all(i)) + EPS)

    def hidden_two(h, i):
        at = slice(i * WIDE, (i + 1) * WIDE)
        a = dot(qx[at, :], u_all(2 * h)) * ratio_out[0:1, halves(h)]
        g = dot(qx[at, :], u_all(2 * h + 1)) * ratio_out[1:2, halves(h)]
        h2[at, halves(h)] = (a * jax.nn.sigmoid(a) * g).astype(BF16)

    def wide_at(i):
        return pl.ds(pl.multiple_of(i * WIDE, WIDE), WIDE)

    def f_copy(i, h):
        piece = (wide_at(i), chunks[4 + h][1])
        return remote(f_out.at[piece], f_in.at[piece], sends["f"], sends["fr"], seq=partner)

    def apply_tile(b, i, h):
        ht = h2[pl.ds(pl.multiple_of(b * rows + i * WIDE, WIDE), WIDE), :]
        f = dot(ht, u_all(4 + h)) * ratio_out[2:3, chunks[4 + h][1]]
        squared = as_row(jnp.sum(f * f, axis=1, keepdims=True))
        where = 0 if b is c else 1
        if h == 0:
            sq[where, :, wide_at(i)] = squared
        else:
            sq[where, :, wide_at(i)] = sq[where, :, wide_at(i)] + squared
        return f

    def apply_out(h):
        for i in range(rows // WIDE):
            f_out[wide_at(i), chunks[4 + h][1]] = apply_tile(oc, i, h).astype(BF16)
            f_copy(i, h).start()

    def apply_own(h):
        for i in range(rows // WIDE):
            branch[wide_at(i), chunks[4 + h][1]] = apply_tile(c, i, h)

    start(x_w)
    for copy in x_k:
        copy.start()
    start(x_e)
    for copy in x_v:
        copy.start()
    start(x_q)
    for j in range(3):
        gather_send(j, 1)

    @pl.when(m == 0)
    def _():
        for x in (kx, vx):
            x[:WINDOW, :] = jnp.zeros((WINDOW, hd), BF16)

    for copy in loads[3:]:
        copy.wait()
    with scope("b_relay0"):
        if line > 2:
            for j in range(3):
                gather_send(j, 2)
    with scope("b_xw"):
        x_w.wait_recv()
    for j in range(3):
        gather_send(3 + j, 1)
    with_next = functools.partial(jnp.logical_and, has_next)
    local_early = with_next(jnp.logical_and(c == 1, m == 0))
    local_late = with_next(jnp.logical_and(c == 1, m > 0))
    passed = with_next(c == 0)
    for copy in halo_k + halo_v:
        start(copy, local_early, False)

    def pass_keys(when):
        for i in range(tiles):
            wait(x_k[i], when)
            start(halo_k[i], jnp.logical_and(passed, when), False)

    def pass_value(i):
        with scope("b_xv"):
            x_v[i].wait_recv()
        start(halo_v[i], passed, False)

    pass_keys(m == 0)
    with scope("b_relay"):
        if line > 2:
            for j in range(3):
                gather_send(3 + j, 2)
        for s in range(3, line):
            for j in range(3):
                gather_send(j, s)
                gather_send(3 + j, s)
    for copy in halo_k + halo_v:
        start(copy, local_late, False)
    with scope("b_xk"):
        pass_keys(m > 0)
    with scope("b_kt"):
        kt[...] = jnp.transpose(kx[WINDOW:, :])
    for i in range(tiles // 2):
        pass_value(i)
    with scope("b_w13"):
        for j in range(2):
            gather_finish(j)
            gather_finish(3 + j)
    with scope("b_fwd_own"):
        forward(c)
    for i in range(tiles // 2, tiles - 1):
        pass_value(i)
    with scope("b_fwd_oc"):
        forward(oc)
    scaled_values(c)
    for j in range(2):
        ratio_out[j:j + 1] = jnp.sqrt(squares(wg[j].reshape(n * shard, hd)))
    with scope("b_w2"):
        gather_finish(2)
        gather_finish(5)
    with scope("b_bwd_own"):
        for h in range(2):
            backward(c, h)
        ratio_out[2:3] = jnp.sqrt(squares(wg[2].reshape(n * shard, hd)))
    x_e.wait_recv()
    pass_value(tiles - 1)
    with scope("b_bwd_oc"):
        scaled_values(oc)
        for h in range(2):
            backward(oc, h)

    for h in range(3):
        with scope("prod%d" % h):
            product(h)
        for i in ((0, 1), (2, 3), (4, 5, 6, 7))[h]:
            for r in range(parts(i)):
                sum_first(i, r)

    def halo_wait():
        for copy in halo_k + halo_v:
            wait(copy, has_prev)

    tasks = (
        [lambda: pl.when(c == 0)(x_q.wait_recv)]
        + [lambda i=i: local_attention(1, i) for i in range(tiles)]
        + [lambda: pl.when(c == 1)(x_q.wait_recv), halo_wait]
        + [lambda i=i: local_attention(0, i) for i in range(tiles)]
        + [lambda i=i: attention_out(i) for i in range(tiles)]
    )
    done = []

    def task():
        if tasks:
            with scope("task%d" % len(done)):
                tasks.pop(0)()
            done.append(0)

    def finished(i):
        set_ratio(i)
        x_g[i].start()
        if i == 1 or i == 3:
            for b in range(2 * rows // WIDE):
                tasks.append(lambda b=b: hidden_two(i // 2, b))

    pieces = [(i, r) for i in range(8) for r in range(parts(i))]
    for p in range(len(pieces) + LAG):
        with scope("p%d" % p):
            if p < len(pieces):
                sum_on(*pieces[p])
            if p >= LAG:
                sum_back(*pieces[p - LAG])
        if p >= LAG:
            i, r = pieces[p - LAG]
            if r == parts(i) - 1:
                finished(i)
                if 4 <= i < 7:
                    while tasks:
                        task()
                    with scope("apply%d" % i):
                        apply_out(i - 4)
                        apply_own(i - 4)
        if p >= FIRST:
            task()

    with scope("t_out"):
        start(x_n)
        apply_out(3)
    mine = []
    for d in range(hn):
        slot = hn - 1 + d
        mine.append(
            remote(
                sq.at[1], sq_in.at[slot], sends["q"], sends["qr"],
                seq=partner, head=lax.rem(hme + d, hn),
            )
        )
    for copy in mine:
        copy.start()
    with scope("t_own"):
        apply_own(3)
    for d in range(1, hn):
        copy = remote(
            sq.at[0], sq_in.at[d - 1], sends["q"], sends["qr"],
            head=lax.rem(hme + d, hn),
        )
        copy.start()
        mine.append(copy)
    with scope("t_outs"):
        x_n.wait_recv()
        for t in range(2):
            group(gis[t], g_r.at[t], g_r.at[t]).wait_recv()
        for i, (j, cols) in enumerate(chunks):
            out = o_all.at[j]
            new = chunk(us, i)[m, c].astype(F32) * ratio_out[j:j + 1, cols]
            out[c, :, cols] = new
            other = chunk(gis, i)[...].astype(F32) * ratio_in[j:j + 1, cols]
            out[oc, :, cols] = other
    stores = [
        pltpu.make_async_copy(o_all.at[j], out, sends["new"])
        for j, out in enumerate((o1_to, o3_to, o2_to))
    ]
    for copy in stores:
        copy.start()
    with scope("t_sends"):
        for copy, when in pending:
            if when is None:
                copy.wait_send()
            else:
                pl.when(when)(copy.wait_send)

        def sent(ref, name, when=None):
            copy = group(ref, sends[name] if isinstance(name, str) else name, sends["ar"])
            if when is None:
                copy.wait_send()
            else:
                pl.when(when)(copy.wait_send)

        for d in range(2):
            for s in range(1, line):
                sent(
                    wg.at[:, 0], ag_s.at[d, s - 1],
                    jnp.logical_and(ahead(d) >= 1, ahead(1 - d) >= s - 1),
                )
        for t, name in enumerate(("a", "b")):
            sent(outs[t], "in_" + name)
            sent(us[t], "out_" + name, edge > 0)
            sent(gis[t], "g_" + name)
        sent(attn_out, "k")
        sent(attn_out, "v")
        sent(kx.at[:WINDOW], "hk", has_next)
        sent(vx.at[:WINDOW], "hv", has_next)
        sent(attn_out, "a")
        sent(f_out, "f")
    with scope("t_sq"):
        total = sq[0]
        group(sq_in, sends["q"], sends["qr"]).wait_recv()
        for slot in range(2 * hn - 1):
            total = total + sq_in[slot]
        group(sq_in, sends["q"], sends["qr"]).wait_send()
        sq[0] = lax.rsqrt(total * (1.0 / (hn * width)) + EPS)

    def tile_store(i, b):
        piece = (tile_at(i), lanes(b))
        return pltpu.make_async_copy(mixed.at[piece], mixed_to.at[piece], sends["mixed"])

    with scope("t_mix"):
        for i in range(tiles):
            at = tile_at(i)
            inv = column(sq[0, 0:1, i * TILE:(i + 1) * TILE])[:, :1]
            own_part = branch[at, :] * inv * gain_in[:, lanes(c)]
            mixed[at, lanes(c)] = (attn[c, at, :] + own_part).astype(BF16)
            tile_store(i, c).start()
            if i == 0:
                group(attn_in, sends["a"], sends["ar"]).wait_recv()
                group(f_in, sends["f"], sends["fr"]).wait_recv()
            other = f_in[at, :].astype(F32) * inv * gain_in[:, lanes(oc)]
            mixed[at, lanes(oc)] = (attn_in[at, :].astype(F32) + other).astype(BF16)
            tile_store(i, oc).start()
    with scope("t_stores"):
        pltpu.make_async_copy(o_all, o_all, sends["new"]).wait()
        pltpu.make_async_copy(mixed, mixed_to, sends["mixed"]).wait()


def store(*refs):
    sems = refs[-1]
    copies = [pltpu.make_async_copy(refs[i], refs[4 + i], sems.at[i]) for i in range(4)]
    for copy in copies:
        copy.start()
    for copy in copies:
        copy.wait()


def local(n, hn, queries, keys, values, rate, fast_gate, fast_up, fast_down, out_gain):
    rows, width = queries.shape
    heads, shard, hd = fast_gate.shape
    line = n // 2
    half = hd // 2
    tiles = rows // TILE
    sums = (4, line, 2, shard, half)
    sums_b = (4, line, 2, shard, hd // 4)
    dma = pltpu.SemaphoreType.DMA
    vmem = pl.BlockSpec(memory_space=pltpu.VMEM)
    hbm = pl.BlockSpec(memory_space=pltpu.HBM)
    results = pl.pallas_call(
        functools.partial(kernel, n, hn),
        out_shape=(
            pltpu.VMEM((rows, width), BF16),
            pltpu.VMEM(fast_gate.shape, F32),
            pltpu.VMEM(fast_up.shape, F32),
            pltpu.VMEM(fast_down.shape, F32),
        ),
        in_specs=[hbm] * 8,
        out_specs=(pl.BlockSpec(memory_space=pl.ANY),) * 4,
        scratch_shapes=[
            pltpu.VMEM((rows, width), BF16),
            pltpu.VMEM((3,) + fast_gate.shape, F32),
            pltpu.VMEM((3, 2, shard, hd), F32),
            pltpu.VMEM(rate.shape, F32),
            pltpu.VMEM((1, width), F32),
            pltpu.VMEM((3, line, 2, shard, hd), BF16),
            pltpu.VMEM(sums, BF16),
            pltpu.VMEM(sums_b, BF16),
            pltpu.VMEM(sums, F32),
            pltpu.VMEM(sums_b, F32),
            pltpu.VMEM(sums, BF16),
            pltpu.VMEM(sums_b, BF16),
            pltpu.VMEM(sums, BF16),
            pltpu.VMEM(sums_b, BF16),
            pltpu.VMEM(sums, BF16),
            pltpu.VMEM(sums_b, BF16),
            pltpu.VMEM((3, shard, hd), BF16),
            pltpu.VMEM((4, shard, half), BF16),
            pltpu.VMEM((4, shard, hd // 4), BF16),
            pltpu.VMEM((8, hd), F32),
            pltpu.VMEM((8, hd), F32),
            pltpu.VMEM((2 * rows, hd), BF16),
            pltpu.VMEM((WINDOW + 2 * rows, hd), BF16),
            pltpu.VMEM((WINDOW + 2 * rows, hd), BF16),
            pltpu.VMEM((hd, 2 * rows), BF16),
            pltpu.VMEM(rate.shape, F32),
            pltpu.VMEM((2 * rows, hd), BF16),
            pltpu.VMEM((2 * rows, hd), BF16),
            pltpu.VMEM((2, 2 * rows, hd), BF16),
            pltpu.VMEM((2, 2 * rows, hd), F32),
            pltpu.VMEM((2, rows, hd), F32),
            pltpu.VMEM((rows, hd), BF16),
            pltpu.VMEM((rows, hd), BF16),
            pltpu.VMEM((2 * rows, hd), BF16),
            pltpu.VMEM((rows, hd), F32),
            pltpu.VMEM((rows, hd), BF16),
            pltpu.VMEM((rows, hd), BF16),
            pltpu.VMEM((2, 8, rows), F32),
            pltpu.VMEM((2 * hn - 1, 8, rows), F32),
        ]
        + [dma((2, line - 1)), dma((2, 6, line - 1))]
        + [dma((4 * math.gcd(PARTS, line) + 4 * math.gcd(PARTS // 2, line),))] * 2
        + [dma((8,)), dma((4,)), dma((4,)), dma((tiles,)), dma((tiles,))]
        + [dma((2 * WINDOW // TILE,)), dma((18,)), dma((2,))],
        compiler_params=pltpu.CompilerParams(
            collective_id=0, has_side_effects=True, vmem_limit_bytes=42 * 1024 * 1024
        ),
        name="ttt_layer",
    )(
        *(
            pltpu.with_memory_space_constraint(x, pltpu.HBM)
            for x in (
                queries, keys, values, rate, out_gain.reshape(1, width),
                fast_gate, fast_up, fast_down,
            )
        )
    )
    return pl.pallas_call(
        store,
        out_shape=tuple(jax.ShapeDtypeStruct(x.shape, x.dtype) for x in results),
        in_specs=[vmem] * 4,
        out_specs=(hbm,) * 4,
        scratch_shapes=[dma((4,))],
        compiler_params=pltpu.CompilerParams(vmem_limit_bytes=1024 * 1024),
        name="store",
    )(*results)


def solution(mesh):
    weights = P("head", "seq", None)
    tokens = P("seq", "head")
    return jax.shard_map(
        functools.partial(local, mesh.shape["seq"], mesh.shape["head"]),
        mesh=mesh,
        in_specs=(tokens, tokens, tokens, P("head", "seq"), weights, weights, weights, P("head")),
        out_specs=(tokens, weights, weights, weights),
        check_vma=False,
    )
```

time: 109 us -> 98.4 us (0.903)
  the two profiles are of different devices: /device:TPU:0 before, /device:TPU:31 now
where the time goes in v2:
time: 98.4 us; the launch traced here: 98.3 us
  Pallas kernels  97.5 us (99%)
    pallas_call x1, Pallas kernels, local(): pl.pallas_call(functools.partial(kernel, n, hn), out_shape=(pltpu.VMEM((r...  96.2 us

profile of v2, /device:TPU:31, one launch (start us, length us, event | category | flops | bytes accessed | tf_op | source)
XLA Modules:
  0.0 98.3 jit_solution(1454198992701305154)
XLA Ops:
  0.6 96.2 %ttt_layer.1 = (bf16[512,1024]{1,0:T(8,128)(2,1)S(1)}, f32[2,64,512]{2,1,0:T(8,128)S(1)}, f32[2,64,512]{2,1,0:T(8,128)S(1)}, f32[2,64,512]{2,1,0:T(8,128)S(1)}) custom-call(bf16[512,1024]{1,0:T(8,128)(2,1)} %q.1, bf16[512,1024]{1,0:T(8,128)(2,1)} %k.1, bf16[512,1024]{1,0:T(8,128)(2,1)} %v.1, f32[2,512]{1,0:T(2,128)} %rate.1, f32[1,1024]{1,0:T(1,128)} %bitcast.1, ...), custom_call_target="tpu_custom_call" | custom-call | tf_op jit(solution)/shard_map/ttt_layer/pallas_call | solution.py:663
  96.8 1.3 %store.1 = (bf16[512,1024]{1,0:T(8,128)(2,1)}, f32[2,64,512]{2,1,0:T(8,128)}, f32[2,64,512]{2,1,0:T(8,128)}, f32[2,64,512]{2,1,0:T(8,128)}) custom-call(bf16[512,1024]{1,0:T(8,128)(2,1)S(1)} %get-tuple-element.8.refs_0_, f32[2,64,512]{2,1,0:T(8,128)S(1)} %get-tuple-element.9.refs_1_, f32[2,64,512]{2,1,0:T(8,128)S(1)} %get-tuple-element.10.refs_2_, ...), custom_call_target="tpu_custom_call" | custom-call | tf_op jit(solution)/shard_map/store/pallas_call | solution.py:731

commit v3 on v2

--- a/solution.py
+++ b/solution.py
@@ -13,8 +13,9 @@
 TILE = 128
 WIDE = 256
 LAG = 3
-FIRST = 1
+FIRST = 2
 PARTS = 4
+BACK = 2
 NONE = -1e30
 MESH = pl.DeviceIdType.MESH
 F32 = jnp.float32
@@ -40,8 +41,9 @@
     mixed_to, o1_to, o3_to, o2_to,
     mixed, o_all, w_in, rate_in, gain_in, wg, ug_a, ug_b, pg_a, pg_b, out_a, out_b, in_a, in_b, ex_a, ex_b, wb_out, gi_a, gi_b,
     ratio_out, ratio_in, qx, kx, vx, kt, eta_x, gv, hid, dab, pre, attn,
+    lse, qn, part_out, part_in, lse_out, lse_in,
     attn_out, attn_in, h2, branch, f_out, f_in, sq, sq_in,
-    ag_s, ag_r, in_r, back_r, l_s, x_s, x_r, k_r, v_r, halo_r, one_s, g_r,
+    ag_s, ag_r, in_r, back_r, l_s, x_s, x_r, k_r, v_r, halo_r, q_r, qb_r, pt_r, one_s, g_r,
 ):
     rows, width = q.shape
     heads, shard, hd = w1.shape
@@ -63,7 +65,7 @@
         name: one_s.at[i]
         for i, name in enumerate(
             ("in_a", "in_b", "out_a", "out_b", "k", "v", "hk", "hv", "g_a", "g_b", "a", "ar",
-             "f", "fr", "q", "qr", "mixed", "new")
+             "f", "fr", "q", "qr", "mixed", "new", "xq", "qb", "pt", "pl")
         )
     }
     us, pgs = (ug_a, ug_b), (pg_a, pg_b)
@@ -174,7 +176,14 @@
     x_k = token_copies(k, kx, "k", k_r)
     x_v = token_copies(v, vx, "v", v_r)
     x_e = to_partner(1, rate, eta_x)
-    x_q = to_partner(2, q.at[:, lanes(oc)], qx.at[block(c)])
+    x_q = [
+        remote(
+            q.at[i * TILE:(i + 1) * TILE, lanes(oc)],
+            qx.at[pl.ds(pl.multiple_of(c * rows + i * TILE, TILE), TILE)],
+            sends["xq"], q_r.at[i], seq=partner,
+        )
+        for i in range(tiles)
+    ]
     x_n = to_partner(3, ratio_out, ratio_in)
     x_g = [
         remote(
@@ -185,6 +194,10 @@
     ]
     has_next = m < line - 1
     has_prev = m > 0
+    asks = jnp.logical_and(has_prev, m >= middle)
+    answers = jnp.logical_and(has_next, m + 1 >= middle)
+    to_other = jnp.logical_and(has_next, jnp.logical_not(answers))
+    takes_all = jnp.logical_and(has_prev, jnp.logical_not(asks))
 
     def halo(x, i, base):
         return remote(
@@ -193,8 +206,27 @@
             sends["hv" if base else "hk"], halo_r.at[base + i], seq=seq_at(m + 1),
         )
 
-    halo_k = [halo(kx, i, 0) for i in range(WINDOW // TILE)]
-    halo_v = [halo(vx, i, WINDOW // TILE) for i in range(WINDOW // TILE)]
+    halo_k = [halo(kx, i, 0) for i in range(tiles)]
+    halo_v = [halo(vx, i, tiles) for i in range(tiles)]
+    back = BACK * TILE
+
+    def back_tile(i):
+        return slice(i * TILE, (i + 1) * TILE)
+
+    q_back = [
+        remote(
+            qx.at[back_tile(i)], qn.at[back_tile(i)], sends["qb"], qb_r.at[i], seq=seq_at(m - 1)
+        )
+        for i in range(BACK)
+    ]
+    part_on = [
+        remote(
+            part_out.at[back_tile(i)], part_in.at[back_tile(i)], sends["pt"], pt_r.at[i],
+            seq=seq_at(m + 1),
+        )
+        for i in range(BACK)
+    ]
+    lse_on = remote(lse_out, lse_in, sends["pl"], pt_r.at[BACK], seq=seq_at(m + 1))
 
     def link(ss, rr, src, dst, d, i, s):
         return remote(
@@ -340,7 +372,9 @@
         top = jnp.max(s, axis=1, keepdims=True)
         e = jnp.exp(s - top)
         total = jnp.sum(e, axis=1, keepdims=True)
-        return (e * (1.0 / total)).astype(BF16)
+        return (e * (1.0 / total)).astype(BF16), top + jnp.log(total)
+
+    first_key = jnp.where(m == 0, WINDOW, jnp.where(asks, back, 0))
 
     def local_attention(b, i):
         span = WINDOW + TILE
@@ -348,17 +382,55 @@
         s = dot_rhs_t(qx[pl.ds(base, TILE), :], kx[pl.ds(base, span), :])
         r = lax.broadcasted_iota(jnp.int32, (TILE, span), 0)
         u = lax.broadcasted_iota(jnp.int32, (TILE, span), 1)
-        ok = (u > r) & (u <= r + WINDOW) & (base + u + m * 2 * rows >= WINDOW)
-        p = softmax(s, ok)
+        ok = (u > r) & (u <= r + WINDOW) & (base + u >= first_key)
+        p, stat = softmax(s, ok)
         attn[b, tile_at(i), :] = dot(p, vx[pl.ds(base, span), :])
+        if b == 0 and i < BACK:
+            lse[back_tile(i), :] = jnp.broadcast_to(stat, (TILE, TILE))
+
+    def next_attention(i):
+        keys = slice(WINDOW + rows + i * TILE, WINDOW + rows + back)
+        span = back - i * TILE
+
+        @pl.when(answers)
+        def _():
+            q_back[i].wait_recv()
+            s = dot_rhs_t(qn[back_tile(i), :], kx[keys, :])
+            r = lax.broadcasted_iota(jnp.int32, (TILE, span), 0)
+            u = lax.broadcasted_iota(jnp.int32, (TILE, span), 1)
+            p, stat = softmax(s, u > r)
+            stat = jnp.where(lax.broadcasted_iota(jnp.int32, stat.shape, 0) < span - 1, stat, NONE)
+            part_out[back_tile(i), :] = dot(p, vx[keys, :]).astype(BF16)
+            lse_out[:, back_tile(i)] = as_row(stat)
+
+        if i == BACK - 1:
+            start(lse_on, answers)
+        start(part_on[i], answers, False)
+
+    def combine(i):
+        at = back_tile(i)
+
+        @pl.when(asks)
+        def _():
+            if i == 0:
+                lse_on.wait_recv()
+            part_on[i].wait_recv()
+            here = lse[at, :1]
+            before = column(lse_in[0:1, at])[:, :1]
+            keep = jax.nn.sigmoid(here - before)
+            attn[0, at, :] = keep * attn[0, at, :] + (1.0 - keep) * part_in[at, :].astype(F32)
 
     def attn_to(i):
         at = slice(i * TILE, (i + 1) * TILE)
         return remote(attn_out.at[at], attn_in.at[at], sends["a"], sends["ar"], seq=partner)
 
-    def attention_out(i):
-        attn_out[i * TILE:(i + 1) * TILE, :] = attn[oc, i * TILE:(i + 1) * TILE, :].astype(BF16)
-        attn_to(i).start()
+    def attention_out(when, some):
+        @pl.when(when)
+        def _():
+            for i in some:
+                at = slice(i * TILE, (i + 1) * TILE)
+                attn_out[at, :] = attn[oc, at, :].astype(BF16)
+                attn_to(i).start()
 
     def squares(x):
         x = x.astype(F32)
@@ -406,11 +478,23 @@
     for copy in x_k:
         copy.start()
     start(x_e)
+    soon = jnp.logical_and(c == 0, asks)
+    for i in range(BACK):
+        start(x_q[i], soon, False)
     for copy in x_v:
         copy.start()
-    start(x_q)
+    for i in range(tiles):
+        if i < BACK:
+            start(x_q[i], jnp.logical_not(soon), False)
+        else:
+            x_q[i].start()
     for j in range(3):
         gather_send(j, 1)
+
+    @pl.when(asks)
+    def _():
+        for x in (kx, vx):
+            x[:back, :] = jnp.zeros((back, hd), BF16)
 
     @pl.when(m == 0)
     def _():
@@ -427,22 +511,22 @@
         x_w.wait_recv()
     for j in range(3):
         gather_send(3 + j, 1)
-    with_next = functools.partial(jnp.logical_and, has_next)
-    local_early = with_next(jnp.logical_and(c == 1, m == 0))
-    local_late = with_next(jnp.logical_and(c == 1, m > 0))
-    passed = with_next(c == 0)
-    for copy in halo_k + halo_v:
-        start(copy, local_early, False)
+    def forward_halo(copies, i, when):
+        sent_on = to_other if i < BACK else has_next
+        start(copies[i], jnp.logical_and(sent_on, when), False)
+
+    for i in range(2 * tiles):
+        forward_halo((halo_k, halo_v)[i // tiles], i % tiles, jnp.logical_and(c == 1, m == 0))
 
     def pass_keys(when):
         for i in range(tiles):
             wait(x_k[i], when)
-            start(halo_k[i], jnp.logical_and(passed, when), False)
+            forward_halo(halo_k, i, jnp.logical_and(c == 0, when))
 
     def pass_value(i):
         with scope("b_xv"):
             x_v[i].wait_recv()
-        start(halo_v[i], passed, False)
+        forward_halo(halo_v, i, c == 0)
 
     pass_keys(m == 0)
     with scope("b_relay"):
@@ -453,10 +537,21 @@
             for j in range(3):
                 gather_send(j, s)
                 gather_send(3 + j, s)
-    for copy in halo_k + halo_v:
-        start(copy, local_late, False)
+    for i in range(2 * tiles):
+        forward_halo((halo_k, halo_v)[i // tiles], i % tiles, jnp.logical_and(c == 1, m > 0))
+    for copy in q_back:
+        start(copy, jnp.logical_and(c == 0, asks), False)
     with scope("b_xk"):
         pass_keys(m > 0)
+    def tokens_in(when, some):
+        for i in some:
+            wait(x_q[i], when)
+
+    with scope("b_qb"):
+        ask = jnp.logical_and(c == 1, asks)
+        tokens_in(ask, range(BACK))
+        for copy in q_back:
+            start(copy, ask, False)
     with scope("b_kt"):
         kt[...] = jnp.transpose(kx[WINDOW:, :])
     for i in range(tiles // 2):
@@ -496,17 +591,39 @@
                 sum_first(i, r)
 
     def halo_wait():
-        for copy in halo_k + halo_v:
-            wait(copy, has_prev)
-
+        for i in range(tiles):
+            for copies in (halo_k, halo_v):
+                wait(
+                    copies[i],
+                    takes_all if i < BACK else has_prev,
+                )
+
+    def first_tokens():
+        tokens_in(c == 0, range(tiles))
+
+    def rest_tokens():
+        tokens_in(jnp.logical_and(c == 1, jnp.logical_not(asks)), range(BACK))
+        tokens_in(c == 1, range(BACK, tiles))
+        halo_wait()
+
+    def attend(b, i):
+        return lambda: local_attention(b, i)
+
+    ones = [attend(1, i) for i in range(tiles)]
+    zeros = [attend(0, i) for i in range(BACK, tiles)] + [attend(0, i) for i in range(BACK)]
     tasks = (
-        [lambda: pl.when(c == 0)(x_q.wait_recv)]
-        + [lambda i=i: local_attention(1, i) for i in range(tiles)]
-        + [lambda: pl.when(c == 1)(x_q.wait_recv), halo_wait]
-        + [lambda i=i: local_attention(0, i) for i in range(tiles)]
-        + [lambda i=i: attention_out(i) for i in range(tiles)]
+        [lambda: (first_tokens(), ones[0]())]
+        + ones[1:]
+        + [lambda: (attention_out(c == 0, range(tiles)), rest_tokens(), zeros[0]())]
+        + zeros[1:]
+        + [lambda: attention_out(c == 1, range(BACK, tiles))]
+        + [lambda i=i: combine(i) for i in range(BACK)]
+        + [lambda: attention_out(c == 1, range(BACK))]
     )
     done = []
+    with scope("b_next"):
+        for i in range(BACK):
+            next_attention(i)
 
     def task():
         if tasks:
@@ -538,7 +655,7 @@
                     with scope("apply%d" % i):
                         apply_out(i - 4)
                         apply_own(i - 4)
-        if p >= FIRST:
+        for _ in range(0 if p < FIRST else 1 if p < len(pieces) - LAG * 2 else 2):
             task()
 
     with scope("t_out"):
@@ -606,8 +723,12 @@
             sent(gis[t], "g_" + name)
         sent(attn_out, "k")
         sent(attn_out, "v")
-        sent(kx.at[:WINDOW], "hk", has_next)
-        sent(vx.at[:WINDOW], "hv", has_next)
+        sent(attn_out, "xq")
+        for x, name in ((kx, "hk"), (vx, "hv")):
+            sent(x.at[:WINDOW], name, to_other)
+            sent(x.at[back:WINDOW], name, answers)
+        sent(part_out, "pt", answers)
+        sent(qn, "qb", asks)
         sent(attn_out, "a")
         sent(f_out, "f")
     with scope("t_sq"):
@@ -702,6 +823,12 @@
             pltpu.VMEM((2, 2 * rows, hd), BF16),
             pltpu.VMEM((2, 2 * rows, hd), F32),
             pltpu.VMEM((2, rows, hd), F32),
+            pltpu.VMEM((BACK * TILE, TILE), F32),
+            pltpu.VMEM((BACK * TILE, hd), BF16),
+            pltpu.VMEM((BACK * TILE, hd), BF16),
+            pltpu.VMEM((BACK * TILE, hd), BF16),
+            pltpu.VMEM((8, BACK * TILE), F32),
+            pltpu.VMEM((8, BACK * TILE), F32),
             pltpu.VMEM((rows, hd), BF16),
             pltpu.VMEM((rows, hd), BF16),
             pltpu.VMEM((2 * rows, hd), BF16),
@@ -714,7 +841,8 @@
         + [dma((2, line - 1)), dma((2, 6, line - 1))]
         + [dma((4 * math.gcd(PARTS, line) + 4 * math.gcd(PARTS // 2, line),))] * 2
         + [dma((8,)), dma((4,)), dma((4,)), dma((tiles,)), dma((tiles,))]
-        + [dma((2 * WINDOW // TILE,)), dma((18,)), dma((2,))],
+        + [dma((2 * WINDOW // TILE,)), dma((tiles,)), dma((BACK,)), dma((BACK + 1,))]
+        + [dma((22,)), dma((2,))],
         compiler_params=pltpu.CompilerParams(
             collective_id=0, has_side_effects=True, vmem_limit_bytes=42 * 1024 * 1024
         ),

time: 98.4 us -> 96.6 us (0.982)
  the two profiles are of different devices: /device:TPU:31 before, /device:TPU:0 now
where the time goes in v3:
time: 96.6 us; the launch traced here: 96.4 us
  Pallas kernels  95.6 us (99%)
    pallas_call x1, Pallas kernels, local(): pl.pallas_call(functools.partial(kernel, n, hn), out_shape=(pltpu.VMEM((r...  94.4 us

profile of v3, /device:TPU:0, one launch (start us, length us, event | category | flops | bytes accessed | tf_op | source)
XLA Modules:
  0.0 96.4 jit_solution(177283757473884023)
XLA Ops:
  0.6 94.4 %ttt_layer.1 = (bf16[512,1024]{1,0:T(8,128)(2,1)S(1)}, f32[2,64,512]{2,1,0:T(8,128)S(1)}, f32[2,64,512]{2,1,0:T(8,128)S(1)}, f32[2,64,512]{2,1,0:T(8,128)S(1)}) custom-call(bf16[512,1024]{1,0:T(8,128)(2,1)} %q.1, bf16[512,1024]{1,0:T(8,128)(2,1)} %k.1, bf16[512,1024]{1,0:T(8,128)(2,1)} %v.1, f32[2,512]{1,0:T(2,128)} %rate.1, f32[1,1024]{1,0:T(1,128)} %bitcast.1, ...), custom_call_target="tpu_custom_call" | custom-call | tf_op jit(solution)/shard_map/ttt_layer/pallas_call | solution.py:784
  95.0 1.3 %store.1 = (bf16[512,1024]{1,0:T(8,128)(2,1)}, f32[2,64,512]{2,1,0:T(8,128)}, f32[2,64,512]{2,1,0:T(8,128)}, f32[2,64,512]{2,1,0:T(8,128)}) custom-call(bf16[512,1024]{1,0:T(8,128)(2,1)S(1)} %get-tuple-element.8.refs_0_, f32[2,64,512]{2,1,0:T(8,128)S(1)} %get-tuple-element.9.refs_1_, f32[2,64,512]{2,1,0:T(8,128)S(1)} %get-tuple-element.10.refs_2_, ...), custom_call_target="tpu_custom_call" | custom-call | tf_op jit(solution)/shard_map/store/pallas_call | solution.py:859

commit v4 on v3

--- a/solution.py
+++ b/solution.py
@@ -41,7 +41,7 @@
     mixed_to, o1_to, o3_to, o2_to,
     mixed, o_all, w_in, rate_in, gain_in, wg, ug_a, ug_b, pg_a, pg_b, out_a, out_b, in_a, in_b, ex_a, ex_b, wb_out, gi_a, gi_b,
     ratio_out, ratio_in, qx, kx, vx, kt, eta_x, gv, hid, dab, pre, attn,
-    lse, qn, part_out, part_in, lse_out, lse_in,
+    inv_all, lse, qn, part_out, part_in, lse_out, lse_in,
     attn_out, attn_in, h2, branch, f_out, f_in, sq, sq_in,
     ag_s, ag_r, in_r, back_r, l_s, x_s, x_r, k_r, v_r, halo_r, q_r, qb_r, pt_r, one_s, g_r,
 ):
@@ -65,7 +65,8 @@
         name: one_s.at[i]
         for i, name in enumerate(
             ("in_a", "in_b", "out_a", "out_b", "k", "v", "hk", "hv", "g_a", "g_b", "a", "ar",
-             "f", "fr", "q", "qr", "mixed", "new", "xq", "qb", "pt", "pl")
+             "f", "fr", "q", "qr", "mixed", "new", "xq", "qb", "pt", "pl",
+             "fr_last")
         )
     }
     us, pgs = (ug_a, ug_b), (pg_a, pg_b)
@@ -346,25 +347,36 @@
                 pre[0, at, halves(h)] = up * g * (1.0 + a * (1.0 - g))
                 pre[1, at, halves(h)] = ag
 
-    def scaled_values(b):
-        eta = column((rate_in if b is c else eta_x)[pl.ds(c, 1), :])[:, :1]
-        vb = vx[after_pad(b), :]
-        gv[block(b), :] = (eta * vb.astype(F32)).astype(BF16)
-
-    def backward(b, h):
-        @pl.loop(0, rows // WIDE)
-        def _(i):
-            at = pl.ds(pl.multiple_of(b * rows + i * WIDE, WIDE), WIDE)
+    def scaled_values(b, i):
+        at = pl.ds(pl.multiple_of(b * rows + i * WIDE, WIDE), WIDE)
+        lane = slice(i * WIDE, (i + 1) * WIDE)
+        eta = column((rate_in if b is c else eta_x)[pl.ds(c, 1), lane])[:, :1]
+        vb = vx[pl.ds(pl.multiple_of(WINDOW + b * rows + i * WIDE, TILE), WIDE), :]
+        gv[at, :] = (eta * vb.astype(F32)).astype(BF16)
+
+    def backward(b, i):
+        scaled_values(b, i)
+        at = pl.ds(pl.multiple_of(b * rows + i * WIDE, WIDE), WIDE)
+        for h in range(2):
             back = dot_rhs_t(gv[at, :], w_rows(2, h))
             dab[h, at, halves(0)] = (back * pre[0, at, halves(h)]).astype(BF16)
             dab[h, at, halves(1)] = (back * pre[1, at, halves(h)]).astype(BF16)
 
-    def product(h):
-        g = dot(kt[...], dab[h]) if h < 2 else dot_lhs_t(hid[...], gv[...])
+    def product(h, top):
+        deep = line // parts(0) * (parts(0) // 2) if parts(0) > 1 else line
+        count = line // deep
+        if top >= count:
+            return
+        size = n * shard // count
+        at_rows = slice(top * size, (top + 1) * size)
+        g = (
+            dot(kt[at_rows, :], dab[h]) if h < 2
+            else dot_lhs_t(hid[:, at_rows], gv[...])
+        )
         for i, at in ((2 * h, 0), (2 * h + 1, half)) if h < 2 else zip(
             range(4, 8), range(0, hd, quarter)
         ):
-            dst = chunk(pgs, i)
+            dst = chunk(pgs, i).at[top * deep:(top + 1) * deep]
             dst[...] = g[:, at:at + dst.shape[-1]].reshape(dst.shape)
 
     def softmax(s, ok):
@@ -452,7 +464,8 @@
 
     def f_copy(i, h):
         piece = (wide_at(i), chunks[4 + h][1])
-        return remote(f_out.at[piece], f_in.at[piece], sends["f"], sends["fr"], seq=partner)
+        arrived = sends["fr" if h < 3 else "fr_last"]
+        return remote(f_out.at[piece], f_in.at[piece], sends["f"], arrived, seq=partner)
 
     def apply_tile(b, i, h):
         ht = h2[pl.ds(pl.multiple_of(b * rows + i * WIDE, WIDE), WIDE), :]
@@ -465,10 +478,15 @@
             sq[where, :, wide_at(i)] = sq[where, :, wide_at(i)] + squared
         return f
 
-    def apply_out(h):
+    def apply_out(h, between=None):
         for i in range(rows // WIDE):
             f_out[wide_at(i), chunks[4 + h][1]] = apply_tile(oc, i, h).astype(BF16)
-            f_copy(i, h).start()
+            if between is None:
+                f_copy(i, h).start()
+        if between is not None:
+            between()
+            for i in range(rows // WIDE):
+                f_copy(i, h).start()
 
     def apply_own(h):
         for i in range(rows // WIDE):
@@ -566,28 +584,33 @@
         pass_value(i)
     with scope("b_fwd_oc"):
         forward(oc)
-    scaled_values(c)
     for j in range(2):
         ratio_out[j:j + 1] = jnp.sqrt(squares(wg[j].reshape(n * shard, hd)))
     with scope("b_w2"):
         gather_finish(2)
         gather_finish(5)
     with scope("b_bwd_own"):
-        for h in range(2):
-            backward(c, h)
+        for i in range(rows // WIDE):
+            backward(c, i)
         ratio_out[2:3] = jnp.sqrt(squares(wg[2].reshape(n * shard, hd)))
     x_e.wait_recv()
+    with scope("b_bwd_oc"):
+        for i in range(rows // WIDE - 1):
+            backward(oc, i)
     pass_value(tiles - 1)
-    with scope("b_bwd_oc"):
-        scaled_values(oc)
-        for h in range(2):
-            backward(oc, h)
+    with scope("b_bwd_last"):
+        backward(oc, rows // WIDE - 1)
 
     for h in range(3):
+        group_of = ((0, 1), (2, 3), (4, 5, 6, 7))[h]
+        sent_first = parts(0) // 2 if h == 0 else 0
         with scope("prod%d" % h):
-            product(h)
-        for i in ((0, 1), (2, 3), (4, 5, 6, 7))[h]:
-            for r in range(parts(i)):
+            product(h, 0)
+            for r in range(sent_first):
+                sum_first(0, r)
+            product(h, 1)
+        for i in group_of:
+            for r in range(sent_first if i == 0 else 0, parts(i)):
                 sum_first(i, r)
 
     def halo_wait():
@@ -658,29 +681,20 @@
         for _ in range(0 if p < FIRST else 1 if p < len(pieces) - LAG * 2 else 2):
             task()
 
+    def square_to(src, slot, **where):
+        return remote(sq.at[src, 0:1], sq_in.at[slot, 0:1], sends["q"], sends["qr"], **where)
+
+    def squares_across():
+        for d in range(hn):
+            square_to(1, hn - 1 + d, seq=partner, head=lax.rem(hme + d, hn)).start()
+
     with scope("t_out"):
         start(x_n)
-        apply_out(3)
-    mine = []
-    for d in range(hn):
-        slot = hn - 1 + d
-        mine.append(
-            remote(
-                sq.at[1], sq_in.at[slot], sends["q"], sends["qr"],
-                seq=partner, head=lax.rem(hme + d, hn),
-            )
-        )
-    for copy in mine:
-        copy.start()
+        apply_out(3, squares_across)
     with scope("t_own"):
         apply_own(3)
-    for d in range(1, hn):
-        copy = remote(
-            sq.at[0], sq_in.at[d - 1], sends["q"], sends["qr"],
-            head=lax.rem(hme + d, hn),
-        )
-        copy.start()
-        mine.append(copy)
+        for d in range(1, hn):
+            square_to(0, d - 1, head=lax.rem(hme + d, hn)).start()
     with scope("t_outs"):
         x_n.wait_recv()
         for t in range(2):
@@ -697,6 +711,39 @@
     ]
     for copy in stores:
         copy.start()
+    every_square = sq_in.at[:, 0:1]
+    with scope("t_sq"):
+        group(every_square, sends["q"], sends["qr"]).wait_recv()
+        total = sq[0, 0:1]
+        for slot in range(2 * hn - 1):
+            total = total + sq_in[slot, 0:1]
+        group(every_square, sends["q"], sends["qr"]).wait_send()
+        inv_row = lax.rsqrt(total * (1.0 / (hn * width)) + EPS)
+        for i in range(tiles):
+            at = slice(i * TILE, (i + 1) * TILE)
+            inv_all[at, :] = column(inv_row[:, at])
+
+    def inverse(at, columns):
+        return jnp.concatenate([inv_all[at, :]] * (columns // TILE), axis=1)
+
+    def tile_store(i, b):
+        piece = (tile_at(i), lanes(b))
+        return pltpu.make_async_copy(mixed.at[piece], mixed_to.at[piece], sends["mixed"])
+
+    def mix_other(i, cols):
+        at = slice(i * TILE, (i + 1) * TILE)
+        first = oc * hd + cols.start
+        to = pl.ds(pl.multiple_of(first, TILE), cols.stop - cols.start)
+        inv = inverse(at, cols.stop - cols.start)
+        other = f_in[at, cols].astype(F32) * inv * gain_in[:, to]
+        mixed[at, to] = (attn_in[at, cols].astype(F32) + other).astype(BF16)
+
+    with scope("t_mix_own"):
+        for i in range(tiles):
+            at = slice(i * TILE, (i + 1) * TILE)
+            own_part = branch[at, :] * inverse(at, hd) * gain_in[:, lanes(c)]
+            mixed[at, lanes(c)] = (attn[c, at, :] + own_part).astype(BF16)
+            tile_store(i, c).start()
     with scope("t_sends"):
         for copy, when in pending:
             if when is None:
@@ -731,30 +778,15 @@
         sent(qn, "qb", asks)
         sent(attn_out, "a")
         sent(f_out, "f")
-    with scope("t_sq"):
-        total = sq[0]
-        group(sq_in, sends["q"], sends["qr"]).wait_recv()
-        for slot in range(2 * hn - 1):
-            total = total + sq_in[slot]
-        group(sq_in, sends["q"], sends["qr"]).wait_send()
-        sq[0] = lax.rsqrt(total * (1.0 / (hn * width)) + EPS)
-
-    def tile_store(i, b):
-        piece = (tile_at(i), lanes(b))
-        return pltpu.make_async_copy(mixed.at[piece], mixed_to.at[piece], sends["mixed"])
-
-    with scope("t_mix"):
+    with scope("t_mix_oc"):
+        group(attn_in, sends["a"], sends["ar"]).wait_recv()
+        group(f_in.at[:, :3 * quarter], sends["f"], sends["fr"]).wait_recv()
         for i in range(tiles):
-            at = tile_at(i)
-            inv = column(sq[0, 0:1, i * TILE:(i + 1) * TILE])[:, :1]
-            own_part = branch[at, :] * inv * gain_in[:, lanes(c)]
-            mixed[at, lanes(c)] = (attn[c, at, :] + own_part).astype(BF16)
-            tile_store(i, c).start()
-            if i == 0:
-                group(attn_in, sends["a"], sends["ar"]).wait_recv()
-                group(f_in, sends["f"], sends["fr"]).wait_recv()
-            other = f_in[at, :].astype(F32) * inv * gain_in[:, lanes(oc)]
-            mixed[at, lanes(oc)] = (attn_in[at, :].astype(F32) + other).astype(BF16)
+            mix_other(i, slice(0, 3 * quarter))
+    with scope("t_last"):
+        group(f_in.at[:, 3 * quarter:], sends["f"], sends["fr_last"]).wait_recv()
+        for i in range(tiles):
+            mix_other(i, slice(3 * quarter, hd))
             tile_store(i, oc).start()
     with scope("t_stores"):
         pltpu.make_async_copy(o_all, o_all, sends["new"]).wait()
@@ -823,6 +855,7 @@
             pltpu.VMEM((2, 2 * rows, hd), BF16),
             pltpu.VMEM((2, 2 * rows, hd), F32),
             pltpu.VMEM((2, rows, hd), F32),
+            pltpu.VMEM((rows, TILE), F32),
             pltpu.VMEM((BACK * TILE, TILE), F32),
             pltpu.VMEM((BACK * TILE, hd), BF16),
             pltpu.VMEM((BACK * TILE, hd), BF16),
@@ -842,7 +875,7 @@
         + [dma((4 * math.gcd(PARTS, line) + 4 * math.gcd(PARTS // 2, line),))] * 2
         + [dma((8,)), dma((4,)), dma((4,)), dma((tiles,)), dma((tiles,))]
         + [dma((2 * WINDOW // TILE,)), dma((tiles,)), dma((BACK,)), dma((BACK + 1,))]
-        + [dma((22,)), dma((2,))],
+        + [dma((23,)), dma((2,))],
         compiler_params=pltpu.CompilerParams(
             collective_id=0, has_side_effects=True, vmem_limit_bytes=42 * 1024 * 1024
         ),

time: 96.6 us -> 93.7 us (0.970)
  Pallas kernels: 95.6 us -> 92.7 us
    pallas_call x1, Pallas kernels: 94.4 us -> 91.5 us  [local(): pl.pallas_call(functools.partial(kernel, n, hn), out_shape=(pltpu.VMEM((r...]
where the time goes in v4:
time: 93.7 us; the launch traced here: 93.5 us
  Pallas kernels  92.7 us (99%)
    pallas_call x1, Pallas kernels, local(): pl.pallas_call(functools.partial(kernel, n, hn), out_shape=(pltpu.VMEM((r...  91.5 us

profile of v4, /device:TPU:0, one launch (start us, length us, event | category | flops | bytes accessed | tf_op | source)
XLA Modules:
  0.0 93.5 jit_solution(16406399939033855484)
XLA Ops:
  0.6 91.5 %ttt_layer.1 = (bf16[512,1024]{1,0:T(8,128)(2,1)S(1)}, f32[2,64,512]{2,1,0:T(8,128)S(1)}, f32[2,64,512]{2,1,0:T(8,128)S(1)}, f32[2,64,512]{2,1,0:T(8,128)S(1)}) custom-call(bf16[512,1024]{1,0:T(8,128)(2,1)} %q.1, bf16[512,1024]{1,0:T(8,128)(2,1)} %k.1, bf16[512,1024]{1,0:T(8,128)(2,1)} %v.1, f32[2,512]{1,0:T(2,128)} %rate.1, f32[1,1024]{1,0:T(1,128)} %bitcast.1, ...), custom_call_target="tpu_custom_call" | custom-call | tf_op jit(solution)/shard_map/ttt_layer/pallas_call | solution.py:816
  92.1 1.3 %store.1 = (bf16[512,1024]{1,0:T(8,128)(2,1)}, f32[2,64,512]{2,1,0:T(8,128)}, f32[2,64,512]{2,1,0:T(8,128)}, f32[2,64,512]{2,1,0:T(8,128)}) custom-call(bf16[512,1024]{1,0:T(8,128)(2,1)S(1)} %get-tuple-element.8.refs_0_, f32[2,64,512]{2,1,0:T(8,128)S(1)} %get-tuple-element.9.refs_1_, f32[2,64,512]{2,1,0:T(8,128)S(1)} %get-tuple-element.10.refs_2_, ...), custom_call_target="tpu_custom_call" | custom-call | tf_op jit(solution)/shard_map/store/pallas_call | solution.py:892

commit v5 on v4

--- a/solution.py
+++ b/solution.py
@@ -15,7 +15,7 @@
 LAG = 3
 FIRST = 2
 PARTS = 4
-BACK = 2
+BACK = 1
 NONE = -1e30
 MESH = pl.DeviceIdType.MESH
 F32 = jnp.float32
@@ -796,7 +796,10 @@
 def store(*refs):
     sems = refs[-1]
     copies = [pltpu.make_async_copy(refs[i], refs[4 + i], sems.at[i]) for i in range(4)]
-    for copy in copies:
+    for at in range(0, refs[0].shape[0], TILE):
+        piece = pl.ds(at, TILE)
+        pltpu.make_async_copy(refs[0].at[piece], refs[4].at[piece], sems.at[0]).start()
+    for copy in copies[1:]:
         copy.start()
     for copy in copies:
         copy.wait()

time: 93.7 us -> 92.9 us (level)
  the two profiles are of different devices: /device:TPU:0 before, /device:TPU:24 now
where the time goes in v5:
time: 92.9 us; the launch traced here: 92.8 us
  Pallas kernels  92 us (99%)
    pallas_call x1, Pallas kernels, local(): pl.pallas_call(functools.partial(kernel, n, hn), out_shape=(pltpu.VMEM((r...  90.7 us

profile of v5, /device:TPU:24, one launch (start us, length us, event | category | flops | bytes accessed | tf_op | source)
XLA Modules:
  0.0 92.8 jit_solution(68579691580745604)
XLA Ops:
  0.6 90.7 %ttt_layer.1 = (bf16[512,1024]{1,0:T(8,128)(2,1)S(1)}, f32[2,64,512]{2,1,0:T(8,128)S(1)}, f32[2,64,512]{2,1,0:T(8,128)S(1)}, f32[2,64,512]{2,1,0:T(8,128)S(1)}) custom-call(bf16[512,1024]{1,0:T(8,128)(2,1)} %q.1, bf16[512,1024]{1,0:T(8,128)(2,1)} %k.1, bf16[512,1024]{1,0:T(8,128)(2,1)} %v.1, f32[2,512]{1,0:T(2,128)} %rate.1, f32[1,1024]{1,0:T(1,128)} %bitcast.1, ...), custom_call_target="tpu_custom_call" | custom-call | tf_op jit(solution)/shard_map/ttt_layer/pallas_call | solution.py:819
  91.3 1.3 %store.1 = (bf16[512,1024]{1,0:T(8,128)(2,1)}, f32[2,64,512]{2,1,0:T(8,128)}, f32[2,64,512]{2,1,0:T(8,128)}, f32[2,64,512]{2,1,0:T(8,128)}) custom-call(bf16[512,1024]{1,0:T(8,128)(2,1)S(1)} %get-tuple-element.8.refs_0_, f32[2,64,512]{2,1,0:T(8,128)S(1)} %get-tuple-element.9.refs_1_, f32[2,64,512]{2,1,0:T(8,128)S(1)} %get-tuple-element.10.refs_2_, ...), custom_call_target="tpu_custom_call" | custom-call | tf_op jit(solution)/shard_map/store/pallas_call | solution.py:895

commit v6 on v5

--- a/solution.py
+++ b/solution.py
@@ -13,6 +13,7 @@
 TILE = 128
 WIDE = 256
 LAG = 3
+SOON = 2
 FIRST = 2
 PARTS = 4
 BACK = 1
@@ -302,19 +303,27 @@
         start(inward_copy(i, r, False), jnp.logical_and(edge > 0, jnp.logical_not(inner)), False)
         start(inward_copy(i, r, True), jnp.logical_and(edge > 0, inner), False)
 
-    def sum_back(i, r):
+    soon_back = jnp.logical_and(inner, left == (c == 0))
+
+    def sum_back(i, r, first):
         j, cols = chunks[i]
         deep = line // parts(i)
-
-        @pl.when(inner)
+        turn = soon_back if first else jnp.logical_and(inner, jnp.logical_not(soon_back))
+
+        @pl.when(turn)
         def _():
             inward_copy(i, r, True).wait_recv()
             total = part(pgs, i, r)[...] + part(exs, i, r)[...].astype(F32)
             old = wg[j, r * deep:(r + 1) * deep, :, :, cols].astype(F32)
             part(us, i, r)[...] = (total + old).astype(BF16)
 
-        wait(outward_copy(i, r), jnp.logical_not(inner))
-        start(outward_copy(i, r), edge > 0, False)
+        if first:
+            start(outward_copy(i, r), jnp.logical_and(edge > 0, soon_back), False)
+        else:
+            wait(outward_copy(i, r), jnp.logical_not(inner))
+            start(
+                outward_copy(i, r), jnp.logical_and(edge > 0, jnp.logical_not(soon_back)), False
+            )
 
     def column(row):
         return jnp.transpose(jnp.broadcast_to(row, (TILE, row.shape[1])))
@@ -666,8 +675,10 @@
         with scope("p%d" % p):
             if p < len(pieces):
                 sum_on(*pieces[p])
+            if 0 <= p - SOON < len(pieces):
+                sum_back(*pieces[p - SOON], True)
             if p >= LAG:
-                sum_back(*pieces[p - LAG])
+                sum_back(*pieces[p - LAG], False)
         if p >= LAG:
             i, r = pieces[p - LAG]
             if r == parts(i) - 1:

time: 92.9 us -> 92.9 us (level)
  the two profiles are of different devices: /device:TPU:24 before, /device:TPU:0 now
where the time goes in v6:
time: 92.9 us; the launch traced here: 92 us
  Pallas kernels  91.2 us (98%)
    pallas_call x1, Pallas kernels, local(): pl.pallas_call(functools.partial(kernel, n, hn), out_shape=(pltpu.VMEM((r...  90 us

profile of v6, /device:TPU:0, one launch (start us, length us, event | category | flops | bytes accessed | tf_op | source)
XLA Modules:
  0.0 92.0 jit_solution(16438537520996348055)
XLA Ops:
  0.6 90.0 %ttt_layer.1 = (bf16[512,1024]{1,0:T(8,128)(2,1)S(1)}, f32[2,64,512]{2,1,0:T(8,128)S(1)}, f32[2,64,512]{2,1,0:T(8,128)S(1)}, f32[2,64,512]{2,1,0:T(8,128)S(1)}) custom-call(bf16[512,1024]{1,0:T(8,128)(2,1)} %q.1, bf16[512,1024]{1,0:T(8,128)(2,1)} %k.1, bf16[512,1024]{1,0:T(8,128)(2,1)} %v.1, f32[2,512]{1,0:T(2,128)} %rate.1, f32[1,1024]{1,0:T(1,128)} %bitcast.1, ...), custom_call_target="tpu_custom_call" | custom-call | tf_op jit(solution)/shard_map/ttt_layer/pallas_call | solution.py:830
  90.6 1.3 %store.1 = (bf16[512,1024]{1,0:T(8,128)(2,1)}, f32[2,64,512]{2,1,0:T(8,128)}, f32[2,64,512]{2,1,0:T(8,128)}, f32[2,64,512]{2,1,0:T(8,128)}) custom-call(bf16[512,1024]{1,0:T(8,128)(2,1)S(1)} %get-tuple-element.8.refs_0_, f32[2,64,512]{2,1,0:T(8,128)S(1)} %get-tuple-element.9.refs_1_, f32[2,64,512]{2,1,0:T(8,128)S(1)} %get-tuple-element.10.refs_2_, ...), custom_call_target="tpu_custom_call" | custom-call | tf_op jit(solution)/shard_map/store/pallas_call | solution.py:906
